TPU v7x, 32 devices: a whole 2x2x4 slice. The times are simulated.
32 devices in a mesh: front: 4 (over z), row: 4 (over x, core), col: 2 (over y).
Axes of the slice: x: 2, y: 2, z: 4, core: 2. Of those that a mesh axis runs over, the one named last changes fastest.
Arguments:
- front_slab: bfloat16 [4, 2048, 8192], P('front', 'row', 'col'), may hold values from -0.0625 to 0.0625
- samples: bfloat16 [8192, 256], P(('row', 'col')), may hold values from -6 to 6
- child_tiles: bfloat16 [64, 128, 2048], P(('front', 'row', 'col')), may hold values from -0.125 to 0.125
- parent_front: int32 [64, 1], P(('front', 'row', 'col')), may hold values from 0 to 3; in each aligned block of 2 rows (0 to 1, 2 to 3, ...) at most 2 rows name the same one
- parent_tile: int32 [64], P(('front', 'row', 'col')), may hold values from 0 to 15
- column_tiles: int32 [64, 16], P(('front', 'row', 'col')), may hold values from 0 to 63
- ranks: int32 [4, 4], P('front', 'row'), may hold values from 128 to 256
Outputs:
- sampled: float32 [4, 2048, 256], P('front', ('row', 'col'))
- bases: float32 [4, 2048, 256], P('front', ('row', 'col'))
Inputs may be any that keep to these rules, and one draw needn't show every extreme that they name: `parent_front`: among the 2 tiles of one device, at most 2 name the same parent front.
All inputs are finite; a program needn't handle non-finite values.
Results may differ from a plain program's by a relative error of at most 0.0003.
Values may be sent and summed in bfloat16 or wider, within the bound.
A program may use at most 64 MiB of HBM per device.

v0:
```python
import functools

import jax
import jax.numpy as jnp
from jax import lax
from jax.experimental import pallas as pl
from jax.experimental.pallas import tpu as pltpu
from jax.sharding import PartitionSpec as P

F32 = jnp.float32
HI = lax.Precision.HIGHEST
LOGICAL = pl.DeviceIdType.MESH


def dot_nt(a, b):
    return lax.dot_general(a, b, (((1,), (1,)), ((), ())), precision=HI, preferred_element_type=F32)


def inverse_factor(a):
    n = a.shape[0]
    tiles = n // 8
    w = [a[8 * t : 8 * t + 8, :] for t in range(tiles)]
    lane = lax.broadcasted_iota(jnp.int32, (8, n), 1)
    sub = lax.broadcasted_iota(jnp.int32, (8, n), 0)
    rows = []
    for t in range(tiles):
        base = 8 * t
        inside = (lane >= base) & (lane < base + 8)
        cols = [jnp.broadcast_to(w[t][:, base + k : base + k + 1], (8, n)) for k in range(8)]
        v = jnp.where(inside, jnp.where(lane - base == sub, 1.0, 0.0), w[t])
        done, pivots = v, cols[0]
        for k in range(8):
            here = sub == k
            pivot = jnp.broadcast_to(cols[k][k : k + 1, :], (8, n))
            inv = 1.0 / pivot
            done = jnp.where(here, v, done)
            pivots = jnp.where(here, pivot, pivots)
            step = jnp.broadcast_to(v[k : k + 1, :], (8, n)) * inv
            v = jnp.where(here, step, v - cols[k] * step)
            for m in range(k + 1, 8):
                step = jnp.broadcast_to(cols[m][k : k + 1, :], (8, n)) * inv
                cols[m] = jnp.where(here, step, cols[m] - cols[k] * step)
        rows.append(jnp.where(lane < base + 8, done, 0.0) * lax.rsqrt(pivots))
        vk = [jnp.broadcast_to(v[k : k + 1, :], (8, n)) for k in range(8)]
        for u in range(t + 1, tiles):
            x = jnp.where(inside, 0.0, w[u])
            terms = [
                jnp.broadcast_to(w[u][:, base + k : base + k + 1], (8, n)) * vk[k] for k in range(8)
            ]
            low = (terms[0] + terms[1]) + (terms[2] + terms[3])
            high = (terms[4] + terms[5]) + (terms[6] + terms[7])
            w[u] = x - (low + high)
    return jnp.concatenate(rows, axis=0)


def basis_kernel(sampled_ref, gram_ref, out_ref, basis_ref):
    half = gram_ref.shape[2]
    rank = gram_ref[0, half : half + 1, :]
    sampled = sampled_ref[...]
    out_ref[...] = sampled
    rows = sampled.shape[0]
    lane = lax.broadcasted_iota(jnp.int32, (rows, half), 1).astype(F32)
    first = jnp.where(lane < rank, sampled[:, :half], 0.0)
    second = jnp.where(lane + half < rank, sampled[:, half:], 0.0)
    r = lax.broadcasted_iota(jnp.int32, (half, half), 0)
    c = lax.broadcasted_iota(jnp.int32, (half, half), 1)
    lane = c.astype(F32)
    a = gram_ref[0, :half, :] + jnp.where((r == c) & (lane >= rank), 1.0, 0.0)
    inv1 = inverse_factor(a)
    low = dot_nt(gram_ref[1, :half, :], inv1)
    a = gram_ref[2, :half, :] + jnp.where((r == c) & (lane + half >= rank), 1.0, 0.0)
    a = a - dot_nt(low, low)
    inv2 = inverse_factor(a)
    basis = dot_nt(first, inv1)
    basis_ref[:, :half] = basis
    basis_ref[:, half:] = dot_nt(second - dot_nt(basis, low), inv2)


def leaf_bases(sampled, gram):
    vmem = pl.BlockSpec(memory_space=pltpu.VMEM)
    return pl.pallas_call(
        basis_kernel,
        out_shape=(jax.ShapeDtypeStruct(sampled.shape, F32),) * 2,
        in_specs=[vmem, vmem],
        out_specs=(vmem, vmem),
        name="leaf_bases",
    )(sampled, gram)


def sample_kernel(
    fronts,
    tile_hbm,
    front_hbm,
    column_hbm,
    rank_hbm,
    slab_ref,
    samples_ref,
    child_ref,
    sampled_ref,
    gram_ref,
    tile_ref,
    front_ref,
    column_ref,
    rank_ref,
    omega,
    slab,
    child,
    held,
    part,
    blocks,
    got1,
    got2,
    gram_own,
    gram_got,
    copy_sem,
    gs,
    gr,
    zs_right,
    zs_left,
    zs_pair,
    zr,
    zr_pair,
    es,
    er,
):
    f, r, c = lax.axis_index("front"), lax.axis_index("row"), lax.axis_index("col")
    x, core = r // 2, r % 2
    width = samples_ref.shape[2]
    half = width // 2
    chunk = samples_ref.shape[0]
    piece = chunk // 4
    odd = f % 2
    count = child_ref.shape[0]
    slab_rows, slab_cols = slab_ref.shape
    own_rows = slab_rows // 2
    pieces = own_rows // 128
    row_tiles = slab_rows * 4 // 128
    r_x = (1 - x) * 2 + core
    r_p = x * 2 + (1 - core)
    to_x, to_y, to_p = (f, r_x, c), (f, r, 1 - c), (f, r_p, c)
    right, left = (f + 1, r, c), (f - 1, r, c)

    loads = [
        pltpu.make_async_copy(child_ref, child, copy_sem.at[0]),
        pltpu.make_async_copy(slab_ref, slab, copy_sem.at[1]),
        pltpu.make_async_copy(
            samples_ref, omega.at[pl.ds((r * 2 + c) * chunk, chunk)], copy_sem.at[2]
        ),
    ]
    small = [
        pltpu.make_async_copy(src, dst, copy_sem.at[3 + n])
        for n, (src, dst) in enumerate(
            (
                (tile_hbm, tile_ref),
                (front_hbm, front_ref),
                (column_hbm, column_ref),
                (rank_hbm, rank_ref),
            )
        )
    ]
    loads[2].start()
    for cp in small:
        cp.start()
    loads[0].start()
    loads[1].start()

    barrier = pltpu.get_barrier_semaphore()
    for target in (to_x, to_y, to_p):
        pl.semaphore_signal(barrier, inc=1, device_id=target, device_id_type=LOGICAL)

    @pl.when(f < fronts - 1)
    def _():
        pl.semaphore_signal(barrier, inc=1, device_id=right, device_id_type=LOGICAL)

    @pl.when(f > 0)
    def _():
        pl.semaphore_signal(barrier, inc=1, device_id=left, device_id_type=LOGICAL)

    pl.semaphore_wait(barrier, 3 + jnp.minimum(f, 1) + jnp.minimum(fronts - 1 - f, 1))

    def rcopy(src, dst, send, recv, target):
        return pltpu.make_async_remote_copy(
            src_ref=src,
            dst_ref=dst,
            send_sem=send,
            recv_sem=recv,
            device_id=target,
            device_id_type=LOGICAL,
        )

    to_z = (f + 1 - 2 * odd, r, c)

    def where_is(row, col, i):
        q = i + odd * (3 - 2 * i)
        return pl.ds((row * 2 + col) * chunk + q * piece, piece)

    sent = []

    def send(place, n, target, src=None):
        src = omega.at[place] if src is None else src
        cp = rcopy(src, omega.at[place], gs.at[n], gr.at[n], target)
        cp.start()
        sent.append(cp)

    def arrived(place, n):
        rcopy(omega.at[place], omega.at[place], gs.at[n], gr.at[n], to_p).wait_recv()

    def own(i):
        return samples_ref.at[pl.ds((i + odd * (3 - 2 * i)) * piece, piece)]

    for i, j in ((0, 1), (1, 0), (2, 2)):
        send(where_is(r, c, i), i, to_x, own(i))
        send(where_is(r, c, j), 3 + j, to_y, own(j))
    for i in range(4):
        send(where_is(r, c, i), 12 + i, to_p, own(i))
    x_at = functools.partial(where_is, r_x, c)
    y_at = functools.partial(where_is, r, 1 - c)
    d_at = functools.partial(where_is, r_x, 1 - c)
    arrived(x_at(0), 0)
    send(x_at(0), 6, to_y)
    send(x_at(0), 8, to_z)
    arrived(y_at(1), 4)
    send(y_at(1), 7, to_x)
    send(x_at(0), 16, to_p)
    send(y_at(1), 21, to_p)
    arrived(y_at(0), 3)
    send(y_at(0), 9, to_z)
    send(y_at(0), 20, to_p)
    arrived(x_at(1), 1)
    send(x_at(1), 17, to_p)
    arrived(x_at(3), 8)
    send(x_at(3), 19, to_p)
    arrived(d_at(0), 6)
    send(d_at(0), 10, to_z)
    send(d_at(0), 24, to_p)
    arrived(d_at(1), 7)
    send(d_at(1), 11, to_z)
    send(d_at(1), 25, to_p)
    arrived(y_at(3), 9)
    send(y_at(3), 23, to_p)
    arrived(x_at(2), 2)
    send(x_at(2), 18, to_p)
    arrived(y_at(2), 5)
    send(y_at(2), 22, to_p)
    arrived(d_at(3), 10)
    send(d_at(3), 27, to_p)
    arrived(d_at(2), 11)
    send(d_at(2), 26, to_p)
    r_d = r_x + r_p - r
    for i in range(4):
        arrived(where_is(r_p, c, i), 12 + i)
        arrived(where_is(r_d, c, i), 16 + i)
        arrived(where_is(r_p, 1 - c, i), 20 + i)
        arrived(where_is(r_d, 1 - c, i), 24 + i)
    for cp in small:
        cp.wait()
    loads[2].wait()
    loads[0].wait()

    def tile_row(p, t):
        return 8 + 64 * (p * count + t)

    group = 2
    labels = jnp.zeros((8, width), F32)
    for t in range(count):
        acc = jnp.zeros((128, width), F32)
        for b in range(0, column_ref.shape[1], group):
            chosen = jnp.concatenate(
                [
                    omega[column_ref[t, b + g]]
                    for g in range(group)
                ],
                axis=0,
            )
            acc = acc + jnp.dot(
                child[t, :, 128 * b : 128 * (b + group)], chosen, preferred_element_type=F32
            )
        for p in range(2):
            at = tile_row(p, t)
            held[0, f, at : at + 64, :] = acc[64 * p : 64 * (p + 1)]
        label = (front_ref[t, 0] * row_tiles + tile_ref[t]).astype(F32)
        labels = jnp.where(lax.broadcasted_iota(jnp.int32, (8, width), 0) == t, label, labels)
    held[0, f, 0:8, :] = labels

    spans = [pl.ds(0, tile_row(1, 0)), pl.ds(tile_row(1, 0), 64 * count)]

    def along(src, p, sem, target):
        ref = held.at[0, src, spans[p]]
        return rcopy(ref, ref, sem.at[p, src], zr.at[p, src], target)

    def across(src, p):
        return rcopy(
            held.at[0, src, spans[p]],
            held.at[1, src, spans[p]],
            zs_pair.at[p, src],
            zr_pair.at[p, src],
            to_p,
        )

    for p in range(2):

        @pl.when(f < fronts - 1)
        def _():
            along(f, p, zs_right, right).start()

        @pl.when(f > 0)
        def _():
            along(f, p, zs_left, left).start()

        across(f, p).start()

    loads[1].wait()

    @pl.loop(0, slab_rows // 128)
    def _(i):
        rows = pl.ds(pl.multiple_of(i * 128, 128), 128)
        part[rows, :] = jnp.dot(
            slab[rows, :],
            omega[pl.ds(c * (slab_cols // 128), slab_cols // 128)].reshape(slab_cols, width),
            preferred_element_type=F32,
        )

    def relay(p):
        for d in range(1, fronts):

            @pl.when(f >= d)
            def _():
                along(f - d, p, zs_right, right).wait_recv()

                @pl.when(f < fronts - 1)
                def _():
                    along(f - d, p, zs_right, right).start()

                across(f - d, p).start()

            @pl.when(f + d < fronts)
            def _():
                along(f + d, p, zs_left, left).wait_recv()

                @pl.when(f > 0)
                def _():
                    along(f + d, p, zs_left, left).start()

                across(f + d, p).start()

        for s in range(fronts):
            across(s, p).wait_recv()

    def fill(p, h, spot, row, col, piece_of_part):
        lanes = slice(h * half, (h + 1) * half)
        first = f * row_tiles + (row * 2 + col) * pieces
        for i in range(pieces):
            wanted = (first + i).astype(F32)
            masks = []
            for side in range(2):
                for s in range(fronts):
                    for t in range(count):
                        label = jnp.broadcast_to(held[side, s, t : t + 1, :half], (8, half))
                        masks.append((side, s, t, label == wanted))

            @pl.loop(0, 2)
            def _(q):
                accs = [jnp.zeros((8, half), F32)] * 4
                if piece_of_part is not None:
                    at = piece_of_part * own_rows + i * 128 + p * 64 + q * 32
                    accs = [part[pl.ds(pl.multiple_of(at + 8 * e, 8), 8), lanes] for e in range(4)]
                for side, s, t, mask in masks:
                    for e in range(4):
                        rows = pl.ds(pl.multiple_of(tile_row(p, t) + q * 32 + 8 * e, 8), 8)
                        accs[e] = accs[e] + jnp.where(mask, held[side, s, rows, lanes], 0.0)
                for e in range(4):
                    rows = pl.ds(pl.multiple_of(i * 64 + q * 32 + 8 * e, 8), 8)
                    blocks[p, h, spot, rows, :] = accs[e]

    two = pl.ds(2, 2)
    first_hop = [
        [
            rcopy(blocks.at[p, h, two], got1.at[p, h], es.at[p, h], er.at[p, h], to)
            for h, to in ((0, to_x), (1, to_y))
        ]
        for p in range(2)
    ]
    second_hop = [
        [
            rcopy(blocks.at[p, h, 1], got2.at[p, h], es.at[p, 2 + h], er.at[p, 2 + h], to)
            for h, to in ((0, to_y), (1, to_x))
        ]
        for p in range(2)
    ]

    def spread(p):
        fill(p, 0, 2, r_x, c, None)
        fill(p, 0, 3, r_x, 1 - c, None)
        first_hop[p][0].start()
        fill(p, 1, 2, r, 1 - c, 1 - c)
        fill(p, 1, 3, r_x, 1 - c, None)
        first_hop[p][1].start()
        fill(p, 0, 1, r, 1 - c, 1 - c)
        fill(p, 1, 1, r_x, c, None)
        fill(p, 0, 0, r, c, c)
        fill(p, 1, 0, r, c, c)

    def forward(p):
        for h in range(2):
            first_hop[p][h].wait_recv()
            blocks[p, h, 1] = blocks[p, h, 1] + got1[p, h, 1]
            second_hop[p][h].start()

    def finish(p):
        for h in range(2):
            second_hop[p][h].wait_recv()
            total = (blocks[p, h, 0] + got1[p, h, 0]) + got2[p, h]
            for i in range(pieces):
                at = i * 128 + p * 64
                sampled_ref[at : at + 64, h * half : (h + 1) * half] = total[64 * i : 64 * (i + 1)]

    relay(0)
    spread(0)
    relay(1)
    forward(0)
    spread(1)
    finish(0)
    forward(1)
    finish(1)
    lane = lax.broadcasted_iota(jnp.int32, (own_rows, half), 1)
    masked = []
    for h in range(2):
        total = sampled_ref[:, h * half : (h + 1) * half]
        masked.append(jnp.where(lane + h * half < rank_ref[0, 0], total, 0.0))
    for n, (i, j) in enumerate(((0, 0), (1, 0), (1, 1))):
        gram_own[n] = lax.dot_general(
            masked[i],
            masked[j],
            (((0,), (0,)), ((), ())),
            precision=HI,
            preferred_element_type=F32,
        )
    g = rcopy(gram_own, gram_got, es.at[0, 4], er.at[0, 4], to_y)
    g.start()
    for cp in sent:
        cp.wait_send()
    for p in range(2):
        for s in range(fronts):
            across(s, p).wait_send()

            @pl.when((f < fronts - 1) & (f >= s))
            def _():
                along(s, p, zs_right, right).wait_send()

            @pl.when((f > 0) & (f <= s))
            def _():
                along(s, p, zs_left, left).wait_send()

        for cp in first_hop[p] + second_hop[p]:
            cp.wait_send()
    g.wait()
    rank = jnp.full((3, 8, half), rank_ref[0, 0].astype(F32), F32)
    gram_ref[:, half : half + 8, :] = rank
    gram_ref[:, :half, :] = gram_own[...] + gram_got[...]


def sampled_and_gram(
    fronts, slab, samples, child_tiles, parent_front, parent_tile, column_tiles, ranks
):
    width = samples.shape[1]
    half = width // 2
    count = child_tiles.shape[0]
    rows = slab.shape[0] // 2
    hbm = pl.BlockSpec(memory_space=pl.ANY)
    vmem = pl.BlockSpec(memory_space=pltpu.VMEM)
    dma = lambda *n: pltpu.SemaphoreType.DMA(n)
    return pl.pallas_call(
        functools.partial(sample_kernel, fronts),
        out_shape=(
            jax.ShapeDtypeStruct((rows, width), F32),
            jax.ShapeDtypeStruct((3, half + 8, half), F32),
        ),
        in_specs=[hbm] * 7,
        out_specs=(vmem, vmem),
        scratch_shapes=[
            pltpu.SMEM(parent_tile.shape, jnp.int32),
            pltpu.SMEM(parent_front.shape, jnp.int32),
            pltpu.SMEM(column_tiles.shape, jnp.int32),
            pltpu.SMEM(ranks.shape, jnp.int32),
            pltpu.VMEM((samples.shape[0] // 128 * 8, 128, width), samples.dtype),
            pltpu.VMEM(slab.shape, slab.dtype),
            pltpu.VMEM(child_tiles.shape, child_tiles.dtype),
            pltpu.VMEM((2, fronts, 128 * count + 8, width), F32),
            pltpu.VMEM((slab.shape[0], width), F32),
            pltpu.VMEM((2, 2, 4, rows // 2, half), F32),
            pltpu.VMEM((2, 2, 2, rows // 2, half), F32),
            pltpu.VMEM((2, 2, rows // 2, half), F32),
            pltpu.VMEM((3, half, half), F32),
            pltpu.VMEM((3, half, half), F32),
            dma(7),
            dma(28),
            dma(28),
            dma(2, fronts),
            dma(2, fronts),
            dma(2, fronts),
            dma(2, fronts),
            dma(2, fronts),
            dma(2, 5),
            dma(2, 5),
        ],
        compiler_params=pltpu.CompilerParams(
            collective_id=0, has_side_effects=True, vmem_limit_bytes=67043328
        ),
        name="sampled_and_gram",
    )(
        parent_tile,
        parent_front,
        column_tiles,
        ranks,
        slab,
        samples.reshape(-1, 128, width),
        child_tiles,
    )


def sampled_and_gram_any(
    slab, samples, child_tiles, parent_front, parent_tile, column_tiles, ranks
):
    width = samples.shape[1]
    half = width // 2
    col_width = slab.shape[1]
    omega = lax.all_gather(samples, ("row", "col"), axis=0, tiled=True)
    own = lax.dynamic_slice_in_dim(omega, lax.axis_index("col") * col_width, col_width, 0)
    direct = lax.psum_scatter(
        jnp.dot(slab, own, preferred_element_type=F32), "col", scatter_dimension=0, tiled=True
    )
    count = child_tiles.shape[0]
    blocks = child_tiles.shape[2] // 128
    chosen = omega.reshape(-1, 128, width)[column_tiles]
    pieces = child_tiles.reshape(count, 128, blocks, 128)
    product = jnp.einsum("trkc,tkcs->trs", pieces, chosen, preferred_element_type=F32)
    row_tiles = slab.shape[0] * lax.axis_size("row") // 128
    label = (parent_front[:, 0] * row_tiles + parent_tile).astype(F32)
    product = lax.all_gather(product, "front", axis=0, tiled=True)
    label = lax.all_gather(label, "front", axis=0, tiled=True)
    wanted = (lax.axis_index("front") * row_tiles + jnp.arange(row_tiles)).astype(F32)
    spread = (label[:, None] == wanted[None, :]).astype(F32)
    rows_full = jnp.einsum("qj,qrs->jrs", spread, product, precision=HI)
    rows_full = rows_full.reshape(row_tiles * 128, width)
    extended = lax.psum_scatter(rows_full, ("row", "col"), scatter_dimension=0, tiled=True)
    sampled = direct + extended
    masked = jnp.where(jnp.arange(width)[None, :] < ranks[0, 0], sampled, 0.0)
    gram = lax.psum(jnp.dot(masked.T, masked, precision=HI), "col")
    gram = jnp.stack([gram[:half, :half], gram[half:, :half], gram[half:, half:]])
    rank = jnp.broadcast_to(ranks.astype(F32)[:, :, None], (3, 8, half))
    return sampled, jnp.concatenate([gram, rank], axis=1)


def on_device(
    sizes, front_slab, samples, child_tiles, parent_front, parent_tile, column_tiles, ranks
):
    args = (samples, child_tiles, parent_front, parent_tile, column_tiles, ranks)
    if sizes["row"] == 4 and sizes["col"] == 2 and sizes["front"] % 2 == 0:
        sampled, gram = sampled_and_gram(sizes["front"], front_slab[0], *args)
    else:
        sampled, gram = sampled_and_gram_any(front_slab[0], *args)
    sampled, basis = leaf_bases(sampled, gram)
    return (sampled[None], basis[None])


def solution(mesh):
    in_specs = (
        P("front", "row", "col"),
        P(("row", "col"), None),
        P(("front", "row", "col"), None, None),
        P(("front", "row", "col"), None),
        P(("front", "row", "col")),
        P(("front", "row", "col"), None),
        P("front", "row"),
    )
    out_specs = (P("front", ("row", "col"), None), P("front", ("row", "col"), None))
    return jax.shard_map(
        functools.partial(on_device, dict(mesh.shape)),
        mesh=mesh,
        in_specs=in_specs,
        out_specs=out_specs,
        check_vma=False,
    )
```

profile of v0, /device:TPU:0, one launch (start us, length us, event | category | flops | bytes accessed | tf_op | source)
XLA Modules:
  0.0 80.2 jit_solution(1434740471251603295)
XLA Ops:
  1.3 1.3 %copy.9.front_hbm = s32[2,1]{1,0:T(2,128)} copy(s32[2,1]{0,1:T(1,128)} %param.10) | data formatting | bytes 16 | tf_op args[3]
  2.6 65.5 %sampled_and_gram.1 = (f32[256,256]{1,0:T(8,128)}, f32[3,136,128]{2,1,0:T(8,128)}) custom-call(s32[2]{0:T(128)} %tile_hbm.1, s32[2,1]{1,0:T(2,128)} %copy.9.front_hbm, s32[2,16]{1,0:T(2,128)} %column_hbm.1, s32[1,1]{1,0:T(1,128)S(6)} %copy.10.rank_hbm, bf16[512,4096]{1,0:T(8,128)(2,1)} %bitcast.4, bf16[8,128,256]{2,1,0:T(8,128)(2,1)} %bitcast.5, ...), custom_call_target="tpu_custom_call" | custom-call | tf_op jit(solution)/shard_map/sampled_and_gram/pallas_call | solution.py:472
  68.1 12.0 %leaf_bases.1 = (f32[256,256]{1,0:T(8,128)}, f32[256,256]{1,0:T(8,128)}) custom-call(f32[256,256]{1,0:T(8,128)} %get-tuple-element.6.sampled_ref, f32[3,136,128]{2,1,0:T(8,128)} %get-tuple-element.7.gram_ref), custom_call_target="tpu_custom_call" | custom-call | tf_op jit(solution)/shard_map/leaf_bases/pallas_call | solution.py:81
where the time goes:
time: 80.3 us; the launch traced here: 80.2 us
  Pallas kernels  77.6 us (97%)
  local copies, waits for them, and re-layouts  1.3 us (2%)
  between operations  1.29 us (2%)
    pallas_call x1, Pallas kernels, sampled_and_gram(): pl.pallas_call(functools.partial(sample_kernel, fronts), out_shape=(jax.S...  65.5 us
    pallas_call x1, Pallas kernels, leaf_bases(): pl.pallas_call(basis_kernel, out_shape=(jax.ShapeDtypeStruct(sampled.shap...  12 us

commit v1 on v0

v1 whole, which is shorter than its diff:
```python
import functools

import jax
import jax.numpy as jnp
from jax import lax
from jax.experimental import pallas as pl
from jax.experimental.pallas import tpu as pltpu
from jax.sharding import PartitionSpec as P

F32 = jnp.float32
HI = lax.Precision.HIGHEST
LOGICAL = pl.DeviceIdType.MESH


def dot_nt(a, b):
    return lax.dot_general(a, b, (((1,), (1,)), ((), ())), precision=HI, preferred_element_type=F32)


def inverse_factor(a):
    n = a.shape[0]
    tiles = n // 8
    w = [a[8 * t : 8 * t + 8, :] for t in range(tiles)]
    lane = lax.broadcasted_iota(jnp.int32, (8, n), 1)
    sub = lax.broadcasted_iota(jnp.int32, (8, n), 0)
    rows = []
    for t in range(tiles):
        base = 8 * t
        inside = (lane >= base) & (lane < base + 8)
        cols = [jnp.broadcast_to(w[t][:, base + k : base + k + 1], (8, n)) for k in range(8)]
        v = jnp.where(inside, jnp.where(lane - base == sub, 1.0, 0.0), w[t])
        done, pivots = v, cols[0]
        for k in range(8):
            here = sub == k
            pivot = jnp.broadcast_to(cols[k][k : k + 1, :], (8, n))
            inv = 1.0 / pivot
            done = jnp.where(here, v, done)
            pivots = jnp.where(here, pivot, pivots)
            step = jnp.broadcast_to(v[k : k + 1, :], (8, n)) * inv
            v = jnp.where(here, step, v - cols[k] * step)
            for m in range(k + 1, 8):
                step = jnp.broadcast_to(cols[m][k : k + 1, :], (8, n)) * inv
                cols[m] = jnp.where(here, step, cols[m] - cols[k] * step)
        rows.append(jnp.where(lane < base + 8, done, 0.0) * lax.rsqrt(pivots))
        vk = [jnp.broadcast_to(v[k : k + 1, :], (8, n)) for k in range(8)]
        for u in range(t + 1, tiles):
            x = jnp.where(inside, 0.0, w[u])
            terms = [
                jnp.broadcast_to(w[u][:, base + k : base + k + 1], (8, n)) * vk[k] for k in range(8)
            ]
            low = (terms[0] + terms[1]) + (terms[2] + terms[3])
            high = (terms[4] + terms[5]) + (terms[6] + terms[7])
            w[u] = x - (low + high)
    return jnp.concatenate(rows, axis=0)


def basis_kernel(sampled_ref, gram_ref, out_ref, basis_ref):
    half = gram_ref.shape[2]
    rank = gram_ref[0, half : half + 1, :]
    sampled = sampled_ref[...]
    out_ref[...] = sampled
    rows = sampled.shape[0]
    lane = lax.broadcasted_iota(jnp.int32, (rows, half), 1).astype(F32)
    first = jnp.where(lane < rank, sampled[:, :half], 0.0)
    second = jnp.where(lane + half < rank, sampled[:, half:], 0.0)
    r = lax.broadcasted_iota(jnp.int32, (half, half), 0)
    c = lax.broadcasted_iota(jnp.int32, (half, half), 1)
    lane = c.astype(F32)
    a = gram_ref[0, :half, :] + jnp.where((r == c) & (lane >= rank), 1.0, 0.0)
    inv1 = inverse_factor(a)
    low = dot_nt(gram_ref[1, :half, :], inv1)
    a = gram_ref[2, :half, :] + jnp.where((r == c) & (lane + half >= rank), 1.0, 0.0)
    a = a - dot_nt(low, low)
    inv2 = inverse_factor(a)
    basis = dot_nt(first, inv1)
    basis_ref[:, :half] = basis
    basis_ref[:, half:] = dot_nt(second - dot_nt(basis, low), inv2)


def leaf_bases(sampled, gram):
    vmem = pl.BlockSpec(memory_space=pltpu.VMEM)
    return pl.pallas_call(
        basis_kernel,
        out_shape=(jax.ShapeDtypeStruct(sampled.shape, F32),) * 2,
        in_specs=[vmem, vmem],
        out_specs=(vmem, vmem),
        name="leaf_bases",
    )(sampled, gram)


LEVELS = 32767.0


def widened(code):
    return code.astype(jnp.int32).astype(F32)


def step_of(code):
    return jnp.exp2(widened(code) * (1.0 / 256.0)) * (1.0 / LEVELS)


def code_of(block):
    peak = jnp.max(jnp.max(jnp.abs(block), axis=0, keepdims=True), axis=1, keepdims=True)
    peak = jnp.broadcast_to(jnp.maximum(peak, 1e-30), (8, 128))
    return jnp.ceil(jnp.log2(peak) * 256.0) + 2.0


def coded(block, code):
    rows, lanes = block.shape
    scale = jnp.exp2(code * (-1.0 / 256.0)) * LEVELS
    scaled = (block.reshape(rows // 8, 8, lanes) * scale[None]).reshape(rows, lanes)
    return jnp.round(scaled).astype(jnp.int32).astype(jnp.int16)


def decoded(words, step):
    rows, lanes = words.shape
    values = widened(words).reshape(rows // 8, 8, lanes) * step[None]
    return values.reshape(rows, lanes)


def sample_kernel(
    fronts,
    tile_hbm,
    front_hbm,
    column_hbm,
    rank_hbm,
    slab_ref,
    samples_ref,
    child_ref,
    sampled_ref,
    gram_ref,
    tile_ref,
    front_ref,
    column_ref,
    rank_ref,
    omega,
    slab,
    child,
    labels,
    label_ref,
    held,
    sums,
    part,
    blocks,
    got,
    gram_own,
    gram_got,
    copy_sem,
    gs,
    gr,
    zs_right,
    zs_left,
    zs_pair,
    zr,
    zr_pair,
    es,
    er,
):
    f, r, c = lax.axis_index("front"), lax.axis_index("row"), lax.axis_index("col")
    x, core = r // 2, r % 2
    width = samples_ref.shape[2]
    half = width // 2
    chunk = samples_ref.shape[0]
    piece = chunk // 8
    odd = f % 2
    count = child_ref.shape[0]
    slab_rows, slab_cols = slab_ref.shape
    own_rows = slab_rows // 2
    pieces = own_rows // 128
    row_tiles = slab_rows * 4 // 128
    head = 8 * count
    r_x = (1 - x) * 2 + core
    r_p = x * 2 + (1 - core)
    r_d = (1 - x) * 2 + (1 - core)
    to_x, to_y, to_p, to_d = (f, r_x, c), (f, r, 1 - c), (f, r_p, c), (f, r_x, 1 - c)
    right, left = (f + 1, r, c), (f - 1, r, c)
    to_z = (f + 1 - 2 * odd, r, c)

    loads = [
        pltpu.make_async_copy(child_ref, child, copy_sem.at[0]),
        pltpu.make_async_copy(slab_ref, slab, copy_sem.at[1]),
        pltpu.make_async_copy(
            samples_ref, omega.at[pl.ds((r * 2 + c) * chunk, chunk)], copy_sem.at[2]
        ),
    ]
    small = [
        pltpu.make_async_copy(src, dst, copy_sem.at[3 + n])
        for n, (src, dst) in enumerate(
            (
                (tile_hbm, tile_ref),
                (front_hbm, front_ref),
                (column_hbm, column_ref),
                (rank_hbm, rank_ref),
            )
        )
    ]
    loads[2].start()
    for cp in small:
        cp.start()
    loads[0].start()
    loads[1].start()

    barrier = pltpu.get_barrier_semaphore()
    for target in (to_x, to_y, to_p, to_d):
        pl.semaphore_signal(barrier, inc=1, device_id=target, device_id_type=LOGICAL)

    @pl.when(f < fronts - 1)
    def _():
        pl.semaphore_signal(barrier, inc=1, device_id=right, device_id_type=LOGICAL)

    @pl.when(f > 0)
    def _():
        pl.semaphore_signal(barrier, inc=1, device_id=left, device_id_type=LOGICAL)

    pl.semaphore_wait(barrier, 4 + jnp.minimum(f, 1) + jnp.minimum(fronts - 1 - f, 1))

    def rcopy(src, dst, send, recv, target):
        return pltpu.make_async_remote_copy(
            src_ref=src,
            dst_ref=dst,
            send_sem=send,
            recv_sem=recv,
            device_id=target,
            device_id_type=LOGICAL,
        )

    def spot(i):
        return (i + odd * (7 - 2 * i)) * piece

    def place(row, col, i):
        return omega.at[pl.ds((row * 2 + col) * chunk + spot(i), piece)]

    sent = []

    def send(ref, n, target, src=None):
        cp = rcopy(ref if src is None else src, ref, gs.at[n], gr.at[n], target)
        cp.start()
        sent.append(cp)

    def arrived(ref, n):
        rcopy(ref, ref, gs.at[n], gr.at[n], to_p).wait_recv()

    def own(i):
        return samples_ref.at[pl.ds(spot(i), piece)]

    x_at = functools.partial(place, r_x, c)
    y_at = functools.partial(place, r, 1 - c)
    d_at = functools.partial(place, r_x, 1 - c)

    for i in range(5):
        send(place(r, c, i), i, to_x, own(i))
        send(place(r, c, 7 - i), 5 + i, to_y, own(7 - i))
    mine = omega.at[pl.ds((r * 2 + c) * chunk, chunk)]
    send(mine, 24, to_p, samples_ref)

    def view(ch, side, src):
        return labels.at[side, src] if ch == 2 else held.at[ch, side, src]

    def along(src, ch, sem, target):
        ref = view(ch, 0, src)
        return rcopy(ref, ref, sem.at[ch, src], zr.at[ch, src], target)

    def across(src, ch):
        return rcopy(
            view(ch, 0, src), view(ch, 1, src), zs_pair.at[ch, src], zr_pair.at[ch, src], to_p
        )

    def launch(ch):
        @pl.when(f < fronts - 1)
        def _():
            along(f, ch, zs_right, right).start()

        @pl.when(f > 0)
        def _():
            along(f, ch, zs_left, left).start()

        across(f, ch).start()

    def relay(ch, d):
        @pl.when(f >= d)
        def _():
            along(f - d, ch, zs_right, right).wait_recv()

            @pl.when(f < fronts - 1)
            def _():
                along(f - d, ch, zs_right, right).start()

            across(f - d, ch).start()

        @pl.when(f + d < fronts)
        def _():
            along(f + d, ch, zs_left, left).wait_recv()

            @pl.when(f > 0)
            def _():
                along(f + d, ch, zs_left, left).start()

            across(f + d, ch).start()

    def paired(ch):
        for s in range(fronts):
            across(s, ch).wait_recv()

    def drained(ch):
        for s in range(fronts):
            across(s, ch).wait_send()

            @pl.when((f < fronts - 1) & (f >= s))
            def _():
                along(s, ch, zs_right, right).wait_send()

            @pl.when((f > 0) & (f <= s))
            def _():
                along(s, ch, zs_left, left).wait_send()

    for cp in small:
        cp.wait()
    at_row = lax.broadcasted_iota(jnp.int32, (8, 128), 0)
    own_labels = jnp.zeros((8, 128), jnp.int32)
    for t in range(count):
        label = front_ref[t] * row_tiles + tile_ref[t]
        own_labels = jnp.where(at_row == t, label, own_labels)
    labels[0, f] = own_labels
    launch(2)

    for i in range(5):
        arrived(x_at(i), i)
        if i < 3:
            send(x_at(i), 18 + i, to_z)
        if i < 4:
            send(x_at(i), 14 + i, to_y)
        send(x_at(i), 25 + i, to_p)
        arrived(y_at(7 - i), 5 + i)
        if i < 3:
            send(y_at(7 - i), 21 + i, to_z)
        if i < 4:
            send(y_at(7 - i), 10 + i, to_x)
        send(y_at(7 - i), 33 + 7 - i, to_p)
        if 1 <= i < fronts:
            relay(2, i)
    for i in range(3):
        arrived(x_at(7 - i), 18 + i)
        send(x_at(7 - i), 25 + 7 - i, to_p)
        arrived(y_at(i), 21 + i)
        send(y_at(i), 33 + i, to_p)
    for d in range(5, fronts):
        relay(2, d)
    paired(2)
    to_smem = pltpu.make_async_copy(labels, label_ref, copy_sem.at[7])
    to_smem.start()
    for i in range(4):
        arrived(d_at(7 - i), 10 + i)
        send(d_at(7 - i), 41 + 7 - i, to_p)
        arrived(d_at(i), 14 + i)
        send(d_at(i), 41 + i, to_p)
    to_smem.wait()

    sources = [(side, s, t) for s in range(fronts) for side in range(2) for t in range(count)]
    none = len(sources)
    known = [label_ref[side, s, t, 0] for side, s, t in sources]
    before = []
    for n, label in enumerate(known):
        prev = jnp.int32(none)
        for m in range(n):
            prev = jnp.where(known[m] == label, m, prev)
        before.append(prev)

    def last_of(row, col, j):
        wanted = f * row_tiles + (row * 2 + col) * pieces + j
        last = jnp.int32(none)
        for n, label in enumerate(known):
            last = jnp.where(label == wanted, n, last)
        return last

    spots = [(r_x, 1 - c), (r_x, c), (r, 1 - c), (r, c)]
    lasts = [[last_of(row, col, j) for j in range(pieces)] for row, col in spots]

    arrived(omega.at[pl.ds((r_p * 2 + c) * chunk, chunk)], 24)
    for i in range(8):
        arrived(place(r_d, c, i), 25 + i)
        arrived(place(r_p, 1 - c, i), 33 + i)
        arrived(place(r_d, 1 - c, i), 41 + i)
    loads[2].wait()
    loads[0].wait()

    group = 2
    products = []
    for t in range(count):
        acc = jnp.zeros((128, width), F32)
        for b in range(0, column_ref.shape[1], group):
            chosen = jnp.concatenate([omega[column_ref[t, b + g]] for g in range(group)], axis=0)
            acc = acc + jnp.dot(
                child[t, :, 128 * b : 128 * (b + group)], chosen, preferred_element_type=F32
            )
        products.append(acc)

    def pack(ref, tiles):
        codes = [code_of(tile) for tile in tiles]
        ref[:head, :] = jnp.concatenate(codes, axis=0).astype(jnp.int32).astype(jnp.int16)
        for t, tile in enumerate(tiles):
            at = head + 128 * t
            ref[at : at + 128, :] = coded(tile, codes[t])

    def unpack(ref, t):
        at = head + 128 * t
        return decoded(ref[at : at + 128, :], step_of(ref[:head, :])[8 * t : 8 * t + 8])

    for h in range(2):
        pack(held.at[h, 0, f], [p[:, h * half : (h + 1) * half] for p in products])
        launch(h)

    loads[1].wait()

    @pl.loop(0, slab_rows // 128)
    def _(i):
        rows = pl.ds(pl.multiple_of(i * 128, 128), 128)
        part[rows, :] = jnp.dot(
            slab[rows, :],
            omega[pl.ds(c * (slab_cols // 128), slab_cols // 128)].reshape(slab_cols, width),
            preferred_element_type=F32,
        )

    sums[none] = jnp.zeros((128, half), F32)

    def accumulate(h):
        for n, (side, s, t) in enumerate(sources):
            sums[n] = unpack(held.at[h, side, s], t) + sums[before[n]]

    def block(h, n, j):
        row, col = spots[n]
        total = sums[lasts[n][j]]
        if n >= 2:
            at = pl.multiple_of(col * own_rows + j * 128, 128)
            total = total + part[pl.ds(at, 128), h * half : (h + 1) * half]
        return total

    def hop(h, n):
        target = (to_d, to_x, to_y)[n]
        return rcopy(blocks.at[h, n], got.at[h, n], es.at[h, n], er.at[h, n], target)

    def spread(h):
        for n in range(3):
            pack(blocks.at[h, n], [block(h, n, j) for j in range(pieces)])
            hop(h, n).start()
        for j in range(pieces):
            sampled_ref[128 * j : 128 * (j + 1), h * half : (h + 1) * half] = block(h, 3, j)

    def finish(h):
        for n in range(3):
            hop(h, n).wait_recv()
        for j in range(pieces):
            total = sampled_ref[128 * j : 128 * (j + 1), h * half : (h + 1) * half]
            for n in range(3):
                total = total + unpack(got.at[h, n], j)
            sampled_ref[128 * j : 128 * (j + 1), h * half : (h + 1) * half] = total

    for d in range(1, fronts):
        relay(0, d)
        if d < fronts - 1:
            relay(1, d)
    paired(0)
    accumulate(0)
    spread(0)
    relay(1, fronts - 1)
    paired(1)
    accumulate(1)
    spread(1)
    finish(0)
    finish(1)
    lane = lax.broadcasted_iota(jnp.int32, (own_rows, half), 1)
    masked = []
    for h in range(2):
        total = sampled_ref[:, h * half : (h + 1) * half]
        masked.append(jnp.where(lane + h * half < rank_ref[0], total, 0.0))
    for n, (i, j) in enumerate(((0, 0), (1, 0), (1, 1))):
        gram_own[n] = lax.dot_general(
            masked[i],
            masked[j],
            (((0,), (0,)), ((), ())),
            precision=HI,
            preferred_element_type=F32,
        )
    g = rcopy(gram_own, gram_got, es.at[0, 3], er.at[0, 3], to_y)
    g.start()
    for cp in sent:
        cp.wait_send()
    for ch in range(3):
        drained(ch)
    for h in range(2):
        for n in range(3):
            hop(h, n).wait_send()
    g.wait()
    rank = jnp.full((3, 8, half), rank_ref[0].astype(F32), F32)
    gram_ref[:, half : half + 8, :] = rank
    gram_ref[:, :half, :] = gram_own[...] + gram_got[...]


def sampled_and_gram(
    fronts, slab, samples, child_tiles, parent_front, parent_tile, column_tiles, ranks
):
    width = samples.shape[1]
    half = width // 2
    count = child_tiles.shape[0]
    rows = slab.shape[0] // 2
    hbm = pl.BlockSpec(memory_space=pl.ANY)
    vmem = pl.BlockSpec(memory_space=pltpu.VMEM)
    dma = lambda *n: pltpu.SemaphoreType.DMA(n)
    parent_front, ranks = parent_front.reshape(-1), ranks.reshape(-1)
    return pl.pallas_call(
        functools.partial(sample_kernel, fronts),
        out_shape=(
            jax.ShapeDtypeStruct((rows, width), F32),
            jax.ShapeDtypeStruct((3, half + 8, half), F32),
        ),
        in_specs=[hbm] * 7,
        out_specs=(vmem, vmem),
        scratch_shapes=[
            pltpu.SMEM(parent_tile.shape, jnp.int32),
            pltpu.SMEM(parent_front.shape, jnp.int32),
            pltpu.SMEM(column_tiles.shape, jnp.int32),
            pltpu.SMEM(ranks.shape, jnp.int32),
            pltpu.VMEM((samples.shape[0] // 128 * 8, 128, width), samples.dtype),
            pltpu.VMEM(slab.shape, slab.dtype),
            pltpu.VMEM(child_tiles.shape, child_tiles.dtype),
            pltpu.VMEM((2, fronts, 8, 128), jnp.int32),
            pltpu.SMEM((2, fronts, 8, 128), jnp.int32),
            pltpu.VMEM((2, 2, fronts, 136 * count, half), jnp.int16),
            pltpu.VMEM((2 * fronts * count + 1, 128, half), F32),
            pltpu.VMEM((slab.shape[0], width), F32),
            pltpu.VMEM((2, 3, 8 * count + rows, half), jnp.int16),
            pltpu.VMEM((2, 3, 8 * count + rows, half), jnp.int16),
            pltpu.VMEM((3, half, half), F32),
            pltpu.VMEM((3, half, half), F32),
            dma(8),
            dma(49),
            dma(49),
            dma(3, fronts),
            dma(3, fronts),
            dma(3, fronts),
            dma(3, fronts),
            dma(3, fronts),
            dma(2, 4),
            dma(2, 4),
        ],
        compiler_params=pltpu.CompilerParams(
            collective_id=0, has_side_effects=True, vmem_limit_bytes=67043328
        ),
        name="sampled_and_gram",
    )(
        parent_tile,
        parent_front,
        column_tiles,
        ranks,
        slab,
        samples.reshape(-1, 128, width),
        child_tiles,
    )


def sampled_and_gram_any(
    slab, samples, child_tiles, parent_front, parent_tile, column_tiles, ranks
):
    width = samples.shape[1]
    half = width // 2
    col_width = slab.shape[1]
    omega = lax.all_gather(samples, ("row", "col"), axis=0, tiled=True)
    own = lax.dynamic_slice_in_dim(omega, lax.axis_index("col") * col_width, col_width, 0)
    direct = lax.psum_scatter(
        jnp.dot(slab, own, preferred_element_type=F32), "col", scatter_dimension=0, tiled=True
    )
    count = child_tiles.shape[0]
    blocks = child_tiles.shape[2] // 128
    chosen = omega.reshape(-1, 128, width)[column_tiles]
    pieces = child_tiles.reshape(count, 128, blocks, 128)
    product = jnp.einsum("trkc,tkcs->trs", pieces, chosen, preferred_element_type=F32)
    row_tiles = slab.shape[0] * lax.axis_size("row") // 128
    label = (parent_front[:, 0] * row_tiles + parent_tile).astype(F32)
    product = lax.all_gather(product, "front", axis=0, tiled=True)
    label = lax.all_gather(label, "front", axis=0, tiled=True)
    wanted = (lax.axis_index("front") * row_tiles + jnp.arange(row_tiles)).astype(F32)
    spread = (label[:, None] == wanted[None, :]).astype(F32)
    rows_full = jnp.einsum("qj,qrs->jrs", spread, product, precision=HI)
    rows_full = rows_full.reshape(row_tiles * 128, width)
    extended = lax.psum_scatter(rows_full, ("row", "col"), scatter_dimension=0, tiled=True)
    sampled = direct + extended
    masked = jnp.where(jnp.arange(width)[None, :] < ranks[0, 0], sampled, 0.0)
    gram = lax.psum(jnp.dot(masked.T, masked, precision=HI), "col")
    gram = jnp.stack([gram[:half, :half], gram[half:, :half], gram[half:, half:]])
    rank = jnp.broadcast_to(ranks.astype(F32)[:, :, None], (3, 8, half))
    return sampled, jnp.concatenate([gram, rank], axis=1)


def on_device(
    sizes, front_slab, samples, child_tiles, parent_front, parent_tile, column_tiles, ranks
):
    args = (samples, child_tiles, parent_front, parent_tile, column_tiles, ranks)
    if sizes["row"] == 4 and sizes["col"] == 2 and sizes["front"] % 2 == 0:
        sampled, gram = sampled_and_gram(sizes["front"], front_slab[0], *args)
    else:
        sampled, gram = sampled_and_gram_any(front_slab[0], *args)
    sampled, basis = leaf_bases(sampled, gram)
    return (sampled[None], basis[None])


def solution(mesh):
    in_specs = (
        P("front", "row", "col"),
        P(("row", "col"), None),
        P(("front", "row", "col"), None, None),
        P(("front", "row", "col"), None),
        P(("front", "row", "col")),
        P(("front", "row", "col"), None),
        P("front", "row"),
    )
    out_specs = (P("front", ("row", "col"), None), P("front", ("row", "col"), None))
    return jax.shard_map(
        functools.partial(on_device, dict(mesh.shape)),
        mesh=mesh,
        in_specs=in_specs,
        out_specs=out_specs,
        check_vma=False,
    )
```

time: 80.3 us -> 63.4 us (0.79)
  Pallas kernels: 77.6 us -> 62 us
  local copies, waits for them, and re-layouts: 1.3 us -> 0 us
    pallas_call x1, Pallas kernels: 65.5 us -> 50 us  [sampled_and_gram(): pl.pallas_call(functools.partial(sample_kernel, fronts), out_shape=(jax.S...]
    unnamed x1 -> x0, local copies, waits for them, and re-layouts: 1.3 us -> none
where the time goes in v1:
time: 63.4 us; the launch traced here: 63.3 us
  Pallas kernels  62 us (98%)
  between operations  1.29 us (2%)
    pallas_call x1, Pallas kernels, sampled_and_gram(): pl.pallas_call(functools.partial(sample_kernel, fronts), out_shape=(jax.S...  50 us
    pallas_call x1, Pallas kernels, leaf_bases(): pl.pallas_call(basis_kernel, out_shape=(jax.ShapeDtypeStruct(sampled.shap...  12 us

profile of v1, /device:TPU:0, one launch (start us, length us, event | category | flops | bytes accessed | tf_op | source)
XLA Modules:
  0.0 63.3 jit_solution(5049387925163747546)
XLA Ops:
  1.3 50.0 %sampled_and_gram.1 = (f32[256,256]{1,0:T(8,128)}, f32[3,136,128]{2,1,0:T(8,128)}) custom-call(s32[2]{0:T(128)} %tile_hbm.1, s32[2]{0:T(128)} %bitcast.9, s32[2,16]{1,0:T(2,128)} %column_hbm.1, s32[1]{0:T(128)} %bitcast.6.rank_hbm, bf16[512,4096]{1,0:T(8,128)(2,1)} %bitcast.7, bf16[8,128,256]{2,1,0:T(8,128)(2,1)} %bitcast.8, bf16[2,128,2048]{2,1,0:T(8,128)(2,1)} %child_ref.1), custom_call_target="tpu_custom_call" | custom-call | tf_op jit(solution)/shard_map/sampled_and_gram/pallas_call | solution.py:508
  51.2 12.0 %leaf_bases.1 = (f32[256,256]{1,0:T(8,128)}, f32[256,256]{1,0:T(8,128)}) custom-call(f32[256,256]{1,0:T(8,128)} %get-tuple-element.6.sampled_ref, f32[3,136,128]{2,1,0:T(8,128)} %get-tuple-element.7.gram_ref), custom_call_target="tpu_custom_call" | custom-call | tf_op jit(solution)/shard_map/leaf_bases/pallas_call | solution.py:81

commit v2 on v1

v2 whole, which is shorter than its diff:
```python
import functools

import jax
import jax.numpy as jnp
from jax import lax
from jax.experimental import pallas as pl
from jax.experimental.pallas import tpu as pltpu
from jax.sharding import PartitionSpec as P

F32 = jnp.float32
HI = lax.Precision.HIGHEST
LOGICAL = pl.DeviceIdType.MESH


def dot_nt(a, b):
    return lax.dot_general(a, b, (((1,), (1,)), ((), ())), precision=HI, preferred_element_type=F32)


def inverse_factor(a):
    n = a.shape[0]
    tiles = n // 8
    w = [a[8 * t : 8 * t + 8, :] for t in range(tiles)]
    lane = lax.broadcasted_iota(jnp.int32, (8, n), 1)
    sub = lax.broadcasted_iota(jnp.int32, (8, n), 0)
    rows = []
    for t in range(tiles):
        base = 8 * t
        inside = (lane >= base) & (lane < base + 8)
        cols = [jnp.broadcast_to(w[t][:, base + k : base + k + 1], (8, n)) for k in range(8)]
        v = jnp.where(inside, jnp.where(lane - base == sub, 1.0, 0.0), w[t])
        done, pivots = v, cols[0]
        for k in range(8):
            here = sub == k
            pivot = jnp.broadcast_to(cols[k][k : k + 1, :], (8, n))
            inv = 1.0 / pivot
            done = jnp.where(here, v, done)
            pivots = jnp.where(here, pivot, pivots)
            step = jnp.broadcast_to(v[k : k + 1, :], (8, n)) * inv
            v = jnp.where(here, step, v - cols[k] * step)
            for m in range(k + 1, 8):
                step = jnp.broadcast_to(cols[m][k : k + 1, :], (8, n)) * inv
                cols[m] = jnp.where(here, step, cols[m] - cols[k] * step)
        rows.append(jnp.where(lane < base + 8, done, 0.0) * lax.rsqrt(pivots))
        vk = [jnp.broadcast_to(v[k : k + 1, :], (8, n)) for k in range(8)]
        for u in range(t + 1, tiles):
            x = jnp.where(inside, 0.0, w[u])
            terms = [
                jnp.broadcast_to(w[u][:, base + k : base + k + 1], (8, n)) * vk[k] for k in range(8)
            ]
            low = (terms[0] + terms[1]) + (terms[2] + terms[3])
            high = (terms[4] + terms[5]) + (terms[6] + terms[7])
            w[u] = x - (low + high)
    return jnp.concatenate(rows, axis=0)


def basis_kernel(sampled_ref, gram_ref, out_ref, basis_ref):
    half = gram_ref.shape[2]
    rank = gram_ref[0, half : half + 1, :]
    sampled = sampled_ref[...]
    out_ref[...] = sampled
    rows = sampled.shape[0]
    lane = lax.broadcasted_iota(jnp.int32, (rows, half), 1).astype(F32)
    first = jnp.where(lane < rank, sampled[:, :half], 0.0)
    second = jnp.where(lane + half < rank, sampled[:, half:], 0.0)
    r = lax.broadcasted_iota(jnp.int32, (half, half), 0)
    c = lax.broadcasted_iota(jnp.int32, (half, half), 1)
    lane = c.astype(F32)
    a = gram_ref[0, :half, :] + jnp.where((r == c) & (lane >= rank), 1.0, 0.0)
    inv1 = inverse_factor(a)
    low = dot_nt(gram_ref[1, :half, :], inv1)
    a = gram_ref[2, :half, :] + jnp.where((r == c) & (lane + half >= rank), 1.0, 0.0)
    a = a - dot_nt(low, low)
    inv2 = inverse_factor(a)
    basis = dot_nt(first, inv1)
    basis_ref[:, :half] = basis
    basis_ref[:, half:] = dot_nt(second - dot_nt(basis, low), inv2)


def leaf_bases(sampled, gram):
    vmem = pl.BlockSpec(memory_space=pltpu.VMEM)
    return pl.pallas_call(
        basis_kernel,
        out_shape=(jax.ShapeDtypeStruct(sampled.shape, F32),) * 2,
        in_specs=[vmem, vmem],
        out_specs=(vmem, vmem),
        name="leaf_bases",
    )(sampled, gram)


LEVELS = 32767.0


def widened(code):
    return code.astype(jnp.int32).astype(F32)


def step_of(code):
    return jnp.exp2(widened(code) * (1.0 / 256.0)) * (1.0 / LEVELS)


def code_of(block):
    peak = jnp.max(jnp.max(jnp.abs(block), axis=0, keepdims=True), axis=1, keepdims=True)
    peak = jnp.broadcast_to(jnp.maximum(peak, 1e-30), (8, 128))
    return jnp.ceil(jnp.log2(peak) * 256.0) + 2.0


def coded(block, code):
    rows, lanes = block.shape
    scale = jnp.exp2(code * (-1.0 / 256.0)) * LEVELS
    scaled = (block.reshape(rows // 8, 8, lanes) * scale[None]).reshape(rows, lanes)
    return jnp.round(scaled).astype(jnp.int32).astype(jnp.int16)


def decoded(words, step):
    rows, lanes = words.shape
    values = widened(words).reshape(rows // 8, 8, lanes) * step[None]
    return values.reshape(rows, lanes)


def sample_kernel(
    tile_hbm,
    front_hbm,
    column_hbm,
    rank_hbm,
    slab_ref,
    samples_ref,
    child_ref,
    sampled_ref,
    basis_ref,
    tile_ref,
    front_ref,
    column_ref,
    rank_ref,
    omega_low,
    omega_high,
    slab,
    child,
    labels,
    label_ref,
    held,
    sums,
    part,
    blocks,
    got,
    gram_own,
    gram_got,
    copy_sem,
    gs,
    gr,
    zs,
    zr,
    es,
    er,
):
    f, r, c = lax.axis_index("front"), lax.axis_index("row"), lax.axis_index("col")
    omega = (omega_low, omega_high)
    x, core = r // 2, r % 2
    width = samples_ref.shape[2]
    half = width // 2
    chunk = samples_ref.shape[0]
    piece = chunk // 8
    odd = f % 2
    count = child_ref.shape[0]
    slab_rows, slab_cols = slab_ref.shape
    own_rows = slab_rows // 2
    pieces = own_rows // 128
    row_tiles = slab_rows * 4 // 128
    head = 8 * count
    r_x = (1 - x) * 2 + core
    r_p = x * 2 + (1 - core)
    r_d = (1 - x) * 2 + (1 - core)
    to_x, to_y, to_p, to_d = (f, r_x, c), (f, r, 1 - c), (f, r_p, c), (f, r_x, 1 - c)
    right, left = (f + 1, r, c), (f - 1, r, c)
    to_z, to_two = (f + 1 - 2 * odd, r, c), ((f + 2) % 4, r, c)
    base = (r * 2 + c) * chunk

    loads = [
        pltpu.make_async_copy(child_ref, child, copy_sem.at[0]),
        pltpu.make_async_copy(slab_ref, slab, copy_sem.at[1]),
    ]
    own_loads = [
        pltpu.make_async_copy(
            samples_ref.at[:, :, pl.ds(h * half, half)],
            omega[h].at[pl.ds(base, chunk)],
            copy_sem.at[8 + h],
        )
        for h in range(2)
    ]
    small = [
        pltpu.make_async_copy(src, dst, copy_sem.at[3 + n])
        for n, (src, dst) in enumerate(
            (
                (tile_hbm, tile_ref),
                (front_hbm, front_ref),
                (column_hbm, column_ref),
                (rank_hbm, rank_ref),
            )
        )
    ]
    for cp in own_loads + small:
        cp.start()
    loads[0].start()
    loads[1].start()

    barrier = pltpu.get_barrier_semaphore()
    for target in (to_x, to_y, to_p, to_d, to_two):
        pl.semaphore_signal(barrier, inc=1, device_id=target, device_id_type=LOGICAL)

    @pl.when(f < 3)
    def _():
        pl.semaphore_signal(barrier, inc=1, device_id=right, device_id_type=LOGICAL)

    @pl.when(f > 0)
    def _():
        pl.semaphore_signal(barrier, inc=1, device_id=left, device_id_type=LOGICAL)

    pl.semaphore_wait(barrier, 5 + jnp.minimum(f, 1) + jnp.minimum(3 - f, 1))

    def rcopy(src, dst, send, recv, target):
        return pltpu.make_async_remote_copy(
            src_ref=src,
            dst_ref=dst,
            send_sem=send,
            recv_sem=recv,
            device_id=target,
            device_id_type=LOGICAL,
        )

    def place(h, row, col, i, n=1):
        start = (row * 2 + col) * chunk + (i + odd * (8 - n - 2 * i)) * piece
        return omega[h].at[pl.ds(start, n * piece)]

    via_z = (3, 1)

    def send(h, ref, n, target):
        rcopy(ref, ref, gs.at[h], gr.at[h, n], target).start()

    def arrived(h, ref, n):
        rcopy(ref, ref, gs.at[h], gr.at[h, n], to_p).wait_recv()

    def all_arrived(h, amount, n):
        arrived(h, omega[h].at[pl.ds(0, amount * piece)], n)

    def pair_up(h, row, col, i, n=1):
        send(h, place(h, row, col, i, n), 12, to_p)

    def gather_own(h):
        own_loads[h].wait()
        for i in range(8 - via_z[h]):
            send(h, place(h, r, c, i), i if i < 4 else 8, to_x)
            send(h, place(h, r, c, 7 - i), 4 + i if i < 4 else 8, to_y)
        pair_up(h, r, c, 0, 8)

    def gather_near(h, i):
        ref = place(h, r_x, c, i)
        arrived(h, ref, i)
        if i < via_z[h]:
            send(h, ref, 9, to_z)
        send(h, ref, 10 + i // 2, to_y)
        pair_up(h, r_x, c, i)
        ref = place(h, r, 1 - c, 7 - i)
        arrived(h, ref, 4 + i)
        if i < via_z[h]:
            send(h, ref, 9, to_z)
        send(h, ref, 10 + i // 2, to_x)
        pair_up(h, r, 1 - c, 7 - i)

    def gather_rest(h):
        n = 4 - via_z[h]
        all_arrived(h, 2 * n, 8)
        pair_up(h, r_x, c, 4, n)
        pair_up(h, r, 1 - c, 4 - n, n)

    def gather_z(h):
        n = via_z[h]
        all_arrived(h, 2 * n, 9)
        pair_up(h, r_x, c, 8 - n, n)
        pair_up(h, r, 1 - c, 0, n)

    def gather_far(h, g):
        all_arrived(h, 4, 10 + g)
        pair_up(h, r_x, 1 - c, 2 * g, 2)
        pair_up(h, r_x, 1 - c, 6 - 2 * g, 2)

    def gather_pair(h):
        all_arrived(h, 32, 12)

    def gather_sent():
        for h in range(2):
            every = omega[h].at[pl.ds(0, 56 * piece)]
            rcopy(every, every, gs.at[h], gr.at[h, 0], to_p).wait_send()

    def view(ch, side, src, n=1):
        if ch == 2:
            return labels.at[side, pl.ds(src, n)]
        return held.at[ch, side, pl.ds(src, n)]

    def along(src, ch, n, target):
        ref = view(ch, 0, src)
        return rcopy(ref, ref, zs.at[ch // 2], zr.at[ch, n], target)

    def across(ch, src, n=1):
        rcopy(view(ch, 0, src, n), view(ch, 1, src, n), zs.at[ch // 2], zr.at[ch, 2], to_p).start()

    def launch(ch):
        @pl.when((f == 0) | (f == 3))
        def _():
            along(f, ch, 1, to_two).start()

        @pl.when((f == 1) | (f == 2))
        def _():
            along(f, ch, 0, to_two).start()

        @pl.when(f < 3)
        def _():
            along(f, ch, 0, right).start()

        @pl.when(f > 0)
        def _():
            along(f, ch, 0, left).start()

        across(ch, f)

    def relay(ch):
        @pl.when(f == 1)
        def _():
            along(3, ch, 1, left).wait_recv()
            along(3, ch, 0, left).start()
            across(ch, 3)

        @pl.when(f == 2)
        def _():
            along(0, ch, 1, right).wait_recv()
            along(0, ch, 0, right).start()
            across(ch, 0)

    def came(ch, amount):
        ref = view(ch, 0, 0, amount)
        rcopy(ref, ref, zs.at[ch // 2], zr.at[ch, 0], to_p).wait_recv()

    def collect(ch):
        @pl.when((f == 0) | (f == 3))
        def _():
            came(ch, 3)
            across(ch, 1 - f // 3, 3)

        @pl.when((f == 1) | (f == 2))
        def _():
            came(ch, 2)
            across(ch, f - 1)
            across(ch, f + 1)

    def paired(ch):
        ref = view(ch, 1, 0, 4)
        rcopy(ref, ref, zs.at[ch // 2], zr.at[ch, 2], to_p).wait_recv()

    def drained():
        def wait(buffer, n, sem):
            ref = buffer.at[..., pl.ds(0, n), :, :]
            rcopy(ref, ref, zs.at[sem], zr.at[0, 0], to_p).wait_send()

        @pl.when((f == 0) | (f == 3))
        def _():
            wait(held, 3, 0)
            wait(labels, 3, 1)

        @pl.when((f == 1) | (f == 2))
        def _():
            wait(held, 4, 0)
            wait(labels, 4, 1)

    gather_own(0)
    for cp in small:
        cp.wait()
    at_row = lax.broadcasted_iota(jnp.int32, (8, 128), 0)
    own_labels = jnp.zeros((8, 128), jnp.int32)
    for t in range(count):
        label = front_ref[t] * row_tiles + tile_ref[t]
        own_labels = jnp.where(at_row == t, label, own_labels)
    labels[0, f] = own_labels
    launch(2)
    for i in range(4):
        gather_near(0, i)
    gather_own(1)
    gather_rest(0)
    relay(2)
    gather_far(0, 0)
    gather_z(0)
    collect(2)
    gather_far(0, 1)
    gather_pair(0)
    loads[0].wait()

    def product(h, t):
        acc = jnp.zeros((128, half), F32)
        for b in range(0, column_ref.shape[1], 2):
            chosen = jnp.concatenate([omega[h][column_ref[t, b + g]] for g in range(2)], axis=0)
            acc = acc + jnp.dot(
                child[t, :, 128 * b : 128 * (b + 2)], chosen, preferred_element_type=F32
            )
        return acc

    def pack(ref, tiles):
        codes = [code_of(tile) for tile in tiles]
        ref[:head, :] = jnp.concatenate(codes, axis=0).astype(jnp.int32).astype(jnp.int16)
        for t, tile in enumerate(tiles):
            at = head + 128 * t
            ref[at : at + 128, :] = coded(tile, codes[t])

    def unpack(ref, t):
        at = head + 128 * t
        return decoded(ref[at : at + 128, :], step_of(ref[:head, :])[8 * t : 8 * t + 8])

    def direct(h):
        @pl.loop(0, slab_rows // 128)
        def _(i):
            rows = pl.ds(pl.multiple_of(i * 128, 128), 128)
            part[h, rows, :] = jnp.dot(
                slab[rows, :],
                omega[h][pl.ds(c * (slab_cols // 128), slab_cols // 128)].reshape(slab_cols, half),
                preferred_element_type=F32,
            )

    pack(held.at[0, 0, f], [product(0, t) for t in range(count)])
    launch(0)
    for i in range(4):
        gather_near(1, i)
    paired(2)
    to_smem = pltpu.make_async_copy(labels, label_ref, copy_sem.at[7])
    to_smem.start()
    loads[1].wait()
    direct(0)
    to_smem.wait()

    sources = [(side, s, t) for s in range(4) for side in range(2) for t in range(count)]
    none = len(sources)
    known = [label_ref[side, s, t, 0] for side, s, t in sources]
    before = []
    for n, label in enumerate(known):
        prev = jnp.int32(none)
        for m in range(n):
            prev = jnp.where(known[m] == label, m, prev)
        before.append(prev)

    def last_of(row, col, j):
        wanted = f * row_tiles + (row * 2 + col) * pieces + j
        last = jnp.int32(none)
        for n, label in enumerate(known):
            last = jnp.where(label == wanted, n, last)
        return last

    spots = [(r_x, 1 - c), (r_x, c), (r, 1 - c), (r, c)]
    lasts = [[last_of(row, col, j) for j in range(pieces)] for row, col in spots]

    gather_rest(1)
    gather_z(1)
    gather_far(1, 0)
    relay(0)
    gather_far(1, 1)
    gather_pair(1)
    pack(held.at[1, 0, f], [product(1, t) for t in range(count)])
    launch(1)
    direct(1)
    sums[none] = jnp.zeros((128, half), F32)

    def accumulate(h):
        for n, (side, s, t) in enumerate(sources):
            sums[n] = unpack(held.at[h, side, s], t) + sums[before[n]]

    def block(h, n, j):
        row, col = spots[n]
        total = sums[lasts[n][j]]
        if n >= 2:
            at = pl.multiple_of(col * own_rows + j * 128, 128)
            total = total + part[h, pl.ds(at, 128), :]
        return total

    def hop(h, n):
        target = (to_d, to_x, to_y)[n]
        return rcopy(blocks.at[h, n], got.at[h, n], es.at[0], er.at[h], target)

    def spread(h):
        for n in range(3):
            pack(blocks.at[h, n], [block(h, n, j) for j in range(pieces)])
            hop(h, n).start()
        for j in range(pieces):
            sampled_ref[128 * j : 128 * (j + 1), h * half : (h + 1) * half] = block(h, 3, j)

    def finish(h):
        rcopy(got.at[h], got.at[h], es.at[0], er.at[h], to_p).wait_recv()
        for j in range(pieces):
            total = sampled_ref[128 * j : 128 * (j + 1), h * half : (h + 1) * half]
            for n in range(3):
                total = total + unpack(got.at[h, n], j)
            sampled_ref[128 * j : 128 * (j + 1), h * half : (h + 1) * half] = total

    def masked(h):
        lane = lax.broadcasted_iota(jnp.int32, (own_rows, half), 1) + h * half
        return jnp.where(lane < rank_ref[0], sampled_ref[:, h * half : (h + 1) * half], 0.0)

    def gram_hop(n):
        return rcopy(gram_own.at[n], gram_got.at[n], es.at[1], er.at[2 + n], to_y)

    def gram_send(n, i, j):
        gram_own[n] = lax.dot_general(
            masked(i),
            masked(j),
            (((0,), (0,)), ((), ())),
            precision=HI,
            preferred_element_type=F32,
        )
        gram_hop(n).start()

    def gram_total(n):
        gram_hop(n).wait_recv()
        total = gram_own[n] + gram_got[n]
        if n == 1:
            return total
        row = lax.broadcasted_iota(jnp.int32, (half, half), 0)
        lane = lax.broadcasted_iota(jnp.int32, (half, half), 1)
        beyond = (row == lane) & (lane + (n // 2) * half >= rank_ref[0])
        return total + jnp.where(beyond, 1.0, 0.0)

    collect(0)
    paired(0)
    accumulate(0)
    spread(0)
    relay(1)
    collect(1)
    paired(1)
    accumulate(1)
    spread(1)
    finish(0)
    gram_send(0, 0, 0)
    finish(1)
    gram_send(1, 1, 0)
    gram_send(2, 1, 1)
    gram = gram_total(0)
    inv1 = inverse_factor(gram)
    low = dot_nt(gram_total(1), inv1)
    inv2 = inverse_factor(gram_total(2) - dot_nt(low, low))
    basis = dot_nt(masked(0), inv1)
    basis_ref[:, :half] = basis
    basis_ref[:, half:] = dot_nt(masked(1) - dot_nt(basis, low), inv2)
    gather_sent()
    drained()
    rcopy(blocks, got, es.at[0], er.at[0], to_p).wait_send()
    rcopy(gram_own, gram_got, es.at[1], er.at[0], to_p).wait_send()


def sampled_and_bases(
    slab, samples, child_tiles, parent_front, parent_tile, column_tiles, ranks
):
    width = samples.shape[1]
    half = width // 2
    count = child_tiles.shape[0]
    rows = slab.shape[0] // 2
    hbm = pl.BlockSpec(memory_space=pl.ANY)
    vmem = pl.BlockSpec(memory_space=pltpu.VMEM)
    dma = lambda *n: pltpu.SemaphoreType.DMA(n)
    parent_front, ranks = parent_front.reshape(-1), ranks.reshape(-1)
    return pl.pallas_call(
        sample_kernel,
        out_shape=(jax.ShapeDtypeStruct((rows, width), F32),) * 2,
        in_specs=[hbm] * 7,
        out_specs=(vmem, vmem),
        scratch_shapes=[
            pltpu.SMEM(parent_tile.shape, jnp.int32),
            pltpu.SMEM(parent_front.shape, jnp.int32),
            pltpu.SMEM(column_tiles.shape, jnp.int32),
            pltpu.SMEM(ranks.shape, jnp.int32),
            pltpu.VMEM((samples.shape[0] // 128 * 8, 128, half), samples.dtype),
            pltpu.VMEM((samples.shape[0] // 128 * 8, 128, half), samples.dtype),
            pltpu.VMEM(slab.shape, slab.dtype),
            pltpu.VMEM(child_tiles.shape, child_tiles.dtype),
            pltpu.VMEM((2, 4, 8, 128), jnp.int32),
            pltpu.SMEM((2, 4, 8, 128), jnp.int32),
            pltpu.VMEM((2, 2, 4, 136 * count, half), jnp.int16),
            pltpu.VMEM((8 * count + 1, 128, half), F32),
            pltpu.VMEM((2, slab.shape[0], half), F32),
            pltpu.VMEM((2, 3, 8 * count + rows, half), jnp.int16),
            pltpu.VMEM((2, 3, 8 * count + rows, half), jnp.int16),
            pltpu.VMEM((3, half, half), F32),
            pltpu.VMEM((3, half, half), F32),
            dma(10),
            dma(2),
            dma(2, 13),
            dma(2),
            dma(3, 3),
            dma(2),
            dma(5),
        ],
        compiler_params=pltpu.CompilerParams(
            collective_id=0, has_side_effects=True, vmem_limit_bytes=48 * 1024 * 1024
        ),
        name="sampled_and_bases",
    )(
        *[
            a if a is ranks else pltpu.with_memory_space_constraint(a, pltpu.HBM)
            for a in (
                parent_tile,
                parent_front,
                column_tiles,
                ranks,
                slab,
                samples.reshape(-1, 128, width),
                child_tiles,
            )
        ]
    )


def sampled_and_gram_any(
    slab, samples, child_tiles, parent_front, parent_tile, column_tiles, ranks
):
    width = samples.shape[1]
    half = width // 2
    col_width = slab.shape[1]
    omega = lax.all_gather(samples, ("row", "col"), axis=0, tiled=True)
    own = lax.dynamic_slice_in_dim(omega, lax.axis_index("col") * col_width, col_width, 0)
    direct = lax.psum_scatter(
        jnp.dot(slab, own, preferred_element_type=F32), "col", scatter_dimension=0, tiled=True
    )
    count = child_tiles.shape[0]
    blocks = child_tiles.shape[2] // 128
    chosen = omega.reshape(-1, 128, width)[column_tiles]
    pieces = child_tiles.reshape(count, 128, blocks, 128)
    product = jnp.einsum("trkc,tkcs->trs", pieces, chosen, preferred_element_type=F32)
    row_tiles = slab.shape[0] * lax.axis_size("row") // 128
    label = (parent_front[:, 0] * row_tiles + parent_tile).astype(F32)
    product = lax.all_gather(product, "front", axis=0, tiled=True)
    label = lax.all_gather(label, "front", axis=0, tiled=True)
    wanted = (lax.axis_index("front") * row_tiles + jnp.arange(row_tiles)).astype(F32)
    spread = (label[:, None] == wanted[None, :]).astype(F32)
    rows_full = jnp.einsum("qj,qrs->jrs", spread, product, precision=HI)
    rows_full = rows_full.reshape(row_tiles * 128, width)
    extended = lax.psum_scatter(rows_full, ("row", "col"), scatter_dimension=0, tiled=True)
    sampled = direct + extended
    masked = jnp.where(jnp.arange(width)[None, :] < ranks[0, 0], sampled, 0.0)
    gram = lax.psum(jnp.dot(masked.T, masked, precision=HI), "col")
    gram = jnp.stack([gram[:half, :half], gram[half:, :half], gram[half:, half:]])
    rank = jnp.broadcast_to(ranks.astype(F32)[:, :, None], (3, 8, half))
    return sampled, jnp.concatenate([gram, rank], axis=1)


def on_device(
    sizes, front_slab, samples, child_tiles, parent_front, parent_tile, column_tiles, ranks
):
    args = (samples, child_tiles, parent_front, parent_tile, column_tiles, ranks)
    tiles, count = samples.shape[0] // 128, child_tiles.shape[0]
    near = sizes["row"] == 4 and sizes["col"] == 2 and sizes["front"] == 4
    if near and tiles % 8 == 0 and count == 2 and front_slab.shape[1] == 512:
        sampled, basis = sampled_and_bases(front_slab[0], *args)
    else:
        sampled, gram = sampled_and_gram_any(front_slab[0], *args)
        sampled, basis = leaf_bases(sampled, gram)
    return (sampled[None], basis[None])


def solution(mesh):
    in_specs = (
        P("front", "row", "col"),
        P(("row", "col"), None),
        P(("front", "row", "col"), None, None),
        P(("front", "row", "col"), None),
        P(("front", "row", "col")),
        P(("front", "row", "col"), None),
        P("front", "row"),
    )
    out_specs = (P("front", ("row", "col"), None), P("front", ("row", "col"), None))
    return jax.shard_map(
        functools.partial(on_device, dict(mesh.shape)),
        mesh=mesh,
        in_specs=in_specs,
        out_specs=out_specs,
        check_vma=False,
    )
```

time: 63.4 us -> 51.4 us (0.81)
  Pallas kernels: 62 us -> 48.5 us
  local copies, waits for them, and re-layouts: 0 us -> 1.41 us
    pallas_call x2 -> x1, Pallas kernels: 62 us -> 48.5 us  [sampled_and_bases(): pl.pallas_call(sample_kernel, out_shape=(jax.ShapeDtypeStruct((rows, widt...]
    unnamed x0 -> x2, local copies, waits for them, and re-layouts: none -> 1.41 us
where the time goes in v2:
time: 51.4 us; the launch traced here: 51.2 us
  Pallas kernels  48.5 us (94%)
  local copies, waits for them, and re-layouts  1.41 us (3%)
  between operations  1.29 us (3%)
    pallas_call x1, Pallas kernels, sampled_and_bases(): pl.pallas_call(sample_kernel, out_shape=(jax.ShapeDtypeStruct((rows, widt...  48.5 us
    unnamed x2, local copies, waits for them, and re-layouts  1.41 us

profile of v2, /device:TPU:0, one launch (start us, length us, event | category | flops | bytes accessed | tf_op | source)
XLA Modules:
  0.0 51.2 jit_solution(794503900431394477)
XLA Ops:
  1.3 48.5 %sampled_and_bases.1 = (f32[256,256]{1,0:T(8,128)S(1)}, f32[256,256]{1,0:T(8,128)S(1)}) custom-call(s32[2]{0:T(128)} %tile_hbm.1, s32[2]{0:T(128)} %bitcast.11, s32[2,16]{1,0:T(2,128)} %column_hbm.1, s32[1]{0:T(128)} %bitcast.6.rank_hbm, bf16[512,4096]{1,0:T(8,128)(2,1)} %bitcast.9, bf16[8,128,256]{2,1,0:T(8,128)(2,1)} %bitcast.10, ...), custom_call_target="tpu_custom_call" | custom-call | tf_op jit(solution)/shard_map/sampled_and_bases/pallas_call | solution.py:562
  49.8 0.7 %copy.12 = f32[1,256,256]{2,1,0:T(8,128)} copy(f32[1,256,256]{2,1,0:T(8,128)S(1)} %bitcast.8) | data formatting | bytes 524288
  50.5 0.7 %copy.13 = f32[1,256,256]{2,1,0:T(8,128)} copy(f32[1,256,256]{2,1,0:T(8,128)S(1)} %bitcast.7) | data formatting | bytes 524288

commit v3 on v2

--- a/solution.py
+++ b/solution.py
@@ -16,40 +16,65 @@
     return lax.dot_general(a, b, (((1,), (1,)), ((), ())), precision=HI, preferred_element_type=F32)
 
 
-def inverse_factor(a):
+def row_of(x, k):
+    return jnp.broadcast_to(x[k : k + 1, :], (8, x.shape[1]))
+def inverse_factor(a, B=2):
     n = a.shape[0]
-    tiles = n // 8
-    w = [a[8 * t : 8 * t + 8, :] for t in range(tiles)]
+    r = lax.broadcasted_iota(jnp.int32, (n, n), 0)
+    l = lax.broadcasted_iota(jnp.int32, (n, n), 1)
+    diagonal = jnp.where(r == l, a, 0.0)
+    across = lax.rsqrt(jnp.sum(diagonal, axis=0, keepdims=True))
+    down = lax.rsqrt(jnp.sum(diagonal, axis=1, keepdims=True))
+    a = a * across * down
+    w = [a[8 * t : 8 * t + 8, :] for t in range(n // 8)]
     lane = lax.broadcasted_iota(jnp.int32, (8, n), 1)
     sub = lax.broadcasted_iota(jnp.int32, (8, n), 0)
+    at = [sub == k for k in range(8)]
+    size = 8 * B
     rows = []
-    for t in range(tiles):
-        base = 8 * t
-        inside = (lane >= base) & (lane < base + 8)
-        cols = [jnp.broadcast_to(w[t][:, base + k : base + k + 1], (8, n)) for k in range(8)]
-        v = jnp.where(inside, jnp.where(lane - base == sub, 1.0, 0.0), w[t])
-        done, pivots = v, cols[0]
-        for k in range(8):
-            here = sub == k
-            pivot = jnp.broadcast_to(cols[k][k : k + 1, :], (8, n))
-            inv = 1.0 / pivot
-            done = jnp.where(here, v, done)
-            pivots = jnp.where(here, pivot, pivots)
-            step = jnp.broadcast_to(v[k : k + 1, :], (8, n)) * inv
-            v = jnp.where(here, step, v - cols[k] * step)
-            for m in range(k + 1, 8):
-                step = jnp.broadcast_to(cols[m][k : k + 1, :], (8, n)) * inv
-                cols[m] = jnp.where(here, step, cols[m] - cols[k] * step)
-        rows.append(jnp.where(lane < base + 8, done, 0.0) * lax.rsqrt(pivots))
-        vk = [jnp.broadcast_to(v[k : k + 1, :], (8, n)) for k in range(8)]
-        for u in range(t + 1, tiles):
-            x = jnp.where(inside, 0.0, w[u])
-            terms = [
-                jnp.broadcast_to(w[u][:, base + k : base + k + 1], (8, n)) * vk[k] for k in range(8)
-            ]
-            low = (terms[0] + terms[1]) + (terms[2] + terms[3])
-            high = (terms[4] + terms[5]) + (terms[6] + terms[7])
-            w[u] = x - (low + high)
+    for first in range(0, n // 8, B):
+        base = 8 * first
+        inside = (lane >= base) & (lane < base + size)
+        mine = w[first : first + B]
+        cols = [[jnp.broadcast_to(x[:, base + k : base + k + 1], (8, n)) for x in mine] for k in range(size)]
+        v = [jnp.where(inside, jnp.where(lane - base - 8 * t == sub, 1.0, 0.0), x) for t, x in enumerate(mine)]
+        done = [None] * B
+        pivots = [None] * B
+        for k in range(0, size, 2):
+            t, s = k // 8, k % 8
+            left, right = cols[k], cols[k + 1]
+            p, q, u = row_of(left[t], s), row_of(right[t], s), row_of(right[t], s + 1)
+            det = p * u - q * q
+            inv = 1.0 / det
+            ratio = 1.0 / p
+            v0, v1 = row_of(v[t], s), row_of(v[t], s + 1)
+            second = v1 - (q * ratio) * v0
+            if s == 0:
+                done[t], pivots[t] = v0, p
+            else:
+                done[t] = jnp.where(at[s], v0, done[t])
+                pivots[t] = jnp.where(at[s], p, pivots[t])
+            done[t] = jnp.where(at[s + 1], second, done[t])
+            pivots[t] = jnp.where(at[s + 1], det * ratio, pivots[t])
+
+            def step(x, x0, x1):
+                y0 = u * x0 - q * x1
+                y1 = p * x1 - q * x0
+                out = [x[i] - (left[i] * y0 + right[i] * y1) * inv for i in range(B)]
+                out[t] = jnp.where(at[s], y0 * inv, jnp.where(at[s + 1], y1 * inv, out[t]))
+                return out
+
+            v = step(v, v0, v1)
+            for m in range(k + 2, size):
+                cols[m] = step(cols[m], row_of(cols[m][t], s), row_of(cols[m][t], s + 1))
+        for t in range(B):
+            rows.append(jnp.where(lane < base + 8 * (t + 1), done[t], 0.0) * lax.rsqrt(pivots[t]) * across)
+        vk = [row_of(v[k // 8], k % 8) for k in range(size)]
+        for i in range(first + B, n // 8):
+            terms = [jnp.broadcast_to(w[i][:, base + k : base + k + 1], (8, n)) * vk[k] for k in range(size)]
+            while len(terms) > 1:
+                terms = [x + y for x, y in zip(terms[::2], terms[1::2])]
+            w[i] = jnp.where(inside, 0.0, w[i]) - terms[0]
     return jnp.concatenate(rows, axis=0)
 
 
@@ -299,13 +324,22 @@
         ref = view(ch, 0, src)
         return rcopy(ref, ref, zs.at[ch // 2], zr.at[ch, n], target)
 
+    def parts(src, ch, n, target):
+        if ch == 2:
+            return [along(src, ch, n, target)]
+        cuts = [pl.ds(0, head + 128), pl.ds(head + 128, 128 * (count - 1))]
+        refs = [held.at[ch, 0, src, cut] for cut in cuts]
+        sems = [zr.at[ch, n + 2 * k if n else 0] for k in range(2)]
+        return [rcopy(a, a, zs.at[0], sem, target) for a, sem in zip(refs, sems)]
+
     def across(ch, src, n=1):
         rcopy(view(ch, 0, src, n), view(ch, 1, src, n), zs.at[ch // 2], zr.at[ch, 2], to_p).start()
 
     def launch(ch):
         @pl.when((f == 0) | (f == 3))
         def _():
-            along(f, ch, 1, to_two).start()
+            for cp in parts(f, ch, 1, to_two):
+                cp.start()
 
         @pl.when((f == 1) | (f == 2))
         def _():
@@ -324,14 +358,16 @@
     def relay(ch):
         @pl.when(f == 1)
         def _():
-            along(3, ch, 1, left).wait_recv()
-            along(3, ch, 0, left).start()
+            for cp, on in zip(parts(3, ch, 1, left), parts(3, ch, 0, left)):
+                cp.wait_recv()
+                on.start()
             across(ch, 3)
 
         @pl.when(f == 2)
         def _():
-            along(0, ch, 1, right).wait_recv()
-            along(0, ch, 0, right).start()
+            for cp, on in zip(parts(0, ch, 1, right), parts(0, ch, 0, right)):
+                cp.wait_recv()
+                on.start()
             across(ch, 0)
 
     def came(ch, amount):
@@ -421,9 +457,10 @@
                 preferred_element_type=F32,
             )
 
+    gather_near(1, 0)
     pack(held.at[0, 0, f], [product(0, t) for t in range(count)])
     launch(0)
-    for i in range(4):
+    for i in range(1, 4):
         gather_near(1, i)
     paired(2)
     to_smem = pltpu.make_async_copy(labels, label_ref, copy_sem.at[7])
@@ -454,13 +491,12 @@
 
     gather_rest(1)
     gather_z(1)
+    relay(0)
     gather_far(1, 0)
-    relay(0)
     gather_far(1, 1)
     gather_pair(1)
     pack(held.at[1, 0, f], [product(1, t) for t in range(count)])
     launch(1)
-    direct(1)
     sums[none] = jnp.zeros((128, half), F32)
 
     def accumulate(h):
@@ -525,6 +561,7 @@
     paired(0)
     accumulate(0)
     spread(0)
+    direct(1)
     relay(1)
     collect(1)
     paired(1)
@@ -586,7 +623,7 @@
             dma(2),
             dma(2, 13),
             dma(2),
-            dma(3, 3),
+            dma(3, 4),
             dma(2),
             dma(5),
         ],

time: 51.4 us -> 49 us (0.953)
  Pallas kernels: 48.5 us -> 46.1 us
    pallas_call x1, Pallas kernels: 48.5 us -> 46.1 us  [sampled_and_bases(): pl.pallas_call(sample_kernel, out_shape=(jax.ShapeDtypeStruct((rows, widt...]
where the time goes in v3:
time: 49 us; the launch traced here: 48.8 us
  Pallas kernels  46.1 us (94%)
  local copies, waits for them, and re-layouts  1.41 us (3%)
  between operations  1.29 us (3%)
    pallas_call x1, Pallas kernels, sampled_and_bases(): pl.pallas_call(sample_kernel, out_shape=(jax.ShapeDtypeStruct((rows, widt...  46.1 us
    unnamed x2, local copies, waits for them, and re-layouts  1.41 us

profile of v3, /device:TPU:0, one launch (start us, length us, event | category | flops | bytes accessed | tf_op | source)
XLA Modules:
  0.0 48.8 jit_solution(2795815218322145708)
XLA Ops:
  1.3 46.1 %sampled_and_bases.1 = (f32[256,256]{1,0:T(8,128)S(1)}, f32[256,256]{1,0:T(8,128)S(1)}) custom-call(s32[2]{0:T(128)} %tile_hbm.1, s32[2]{0:T(128)} %bitcast.11, s32[2,16]{1,0:T(2,128)} %column_hbm.1, s32[1]{0:T(128)} %bitcast.6.rank_hbm, bf16[512,4096]{1,0:T(8,128)(2,1)} %bitcast.9, bf16[8,128,256]{2,1,0:T(8,128)(2,1)} %bitcast.10, ...), custom_call_target="tpu_custom_call" | custom-call | tf_op jit(solution)/shard_map/sampled_and_bases/pallas_call | solution.py:599
  47.4 0.7 %copy.12 = f32[1,256,256]{2,1,0:T(8,128)} copy(f32[1,256,256]{2,1,0:T(8,128)S(1)} %bitcast.8) | data formatting | bytes 524288
  48.1 0.7 %copy.13 = f32[1,256,256]{2,1,0:T(8,128)} copy(f32[1,256,256]{2,1,0:T(8,128)S(1)} %bitcast.7) | data formatting | bytes 524288

commit v4 on v3

--- a/solution.py
+++ b/solution.py
@@ -146,16 +146,14 @@
     tile_hbm,
     front_hbm,
     column_hbm,
-    rank_hbm,
+    rank_ref,
     slab_ref,
     samples_ref,
     child_ref,
-    sampled_ref,
-    basis_ref,
+    out_ref,
     tile_ref,
     front_ref,
     column_ref,
-    rank_ref,
     omega_low,
     omega_high,
     slab,
@@ -179,6 +177,7 @@
 ):
     f, r, c = lax.axis_index("front"), lax.axis_index("row"), lax.axis_index("col")
     omega = (omega_low, omega_high)
+    sampled_ref, basis_ref = out_ref.at[0], out_ref.at[1]
     x, core = r // 2, r % 2
     width = samples_ref.shape[2]
     half = width // 2
@@ -218,7 +217,6 @@
                 (tile_hbm, tile_ref),
                 (front_hbm, front_ref),
                 (column_hbm, column_ref),
-                (rank_hbm, rank_ref),
             )
         )
     ]
@@ -447,8 +445,8 @@
         at = head + 128 * t
         return decoded(ref[at : at + 128, :], step_of(ref[:head, :])[8 * t : 8 * t + 8])
 
-    def direct(h):
-        @pl.loop(0, slab_rows // 128)
+    def direct(h, low, high):
+        @pl.loop(low, high)
         def _(i):
             rows = pl.ds(pl.multiple_of(i * 128, 128), 128)
             part[h, rows, :] = jnp.dot(
@@ -466,7 +464,7 @@
     to_smem = pltpu.make_async_copy(labels, label_ref, copy_sem.at[7])
     to_smem.start()
     loads[1].wait()
-    direct(0)
+    direct(0, 0, slab_rows // 128)
     to_smem.wait()
 
     sources = [(side, s, t) for s in range(4) for side in range(2) for t in range(count)]
@@ -561,8 +559,9 @@
     paired(0)
     accumulate(0)
     spread(0)
-    direct(1)
+    direct(1, 0, slab_rows // 256)
     relay(1)
+    direct(1, slab_rows // 256, slab_rows // 128)
     collect(1)
     paired(1)
     accumulate(1)
@@ -572,13 +571,13 @@
     finish(1)
     gram_send(1, 1, 0)
     gram_send(2, 1, 1)
-    gram = gram_total(0)
-    inv1 = inverse_factor(gram)
+    inv1 = inverse_factor(gram_total(0))
     low = dot_nt(gram_total(1), inv1)
-    inv2 = inverse_factor(gram_total(2) - dot_nt(low, low))
+    gram = gram_total(2) - dot_nt(low, low)
     basis = dot_nt(masked(0), inv1)
     basis_ref[:, :half] = basis
-    basis_ref[:, half:] = dot_nt(masked(1) - dot_nt(basis, low), inv2)
+    rest = masked(1) - dot_nt(basis, low)
+    basis_ref[:, half:] = dot_nt(rest, inverse_factor(gram))
     gather_sent()
     drained()
     rcopy(blocks, got, es.at[0], er.at[0], to_p).wait_send()
@@ -598,14 +597,13 @@
     parent_front, ranks = parent_front.reshape(-1), ranks.reshape(-1)
     return pl.pallas_call(
         sample_kernel,
-        out_shape=(jax.ShapeDtypeStruct((rows, width), F32),) * 2,
-        in_specs=[hbm] * 7,
-        out_specs=(vmem, vmem),
+        out_shape=jax.ShapeDtypeStruct((2, rows, width), F32),
+        in_specs=[hbm] * 3 + [pl.BlockSpec(memory_space=pltpu.SMEM)] + [hbm] * 3,
+        out_specs=vmem,
         scratch_shapes=[
             pltpu.SMEM(parent_tile.shape, jnp.int32),
             pltpu.SMEM(parent_front.shape, jnp.int32),
             pltpu.SMEM(column_tiles.shape, jnp.int32),
-            pltpu.SMEM(ranks.shape, jnp.int32),
             pltpu.VMEM((samples.shape[0] // 128 * 8, 128, half), samples.dtype),
             pltpu.VMEM((samples.shape[0] // 128 * 8, 128, half), samples.dtype),
             pltpu.VMEM(slab.shape, slab.dtype),

time: 49 us -> 48.3 us (0.986)
  local copies, waits for them, and re-layouts: 1.41 us -> 0.82 us
    unnamed x2 -> x0, local copies, waits for them, and re-layouts: 1.41 us -> none
    another operation x0 -> x1, local copies, waits for them, and re-layouts: none -> 0.82 us  [on_device(): sampled, basis = sampled_and_bases(front_slab[0], *args)]
where the time goes in v4:
time: 48.3 us; the launch traced here: 48.1 us
  Pallas kernels  46 us (95%)
  between operations  1.29 us (3%)
  local copies, waits for them, and re-layouts  0.82 us (2%)
    pallas_call x1, Pallas kernels, sampled_and_bases(): pl.pallas_call(sample_kernel, out_shape=jax.ShapeDtypeStruct((2, rows, wi...  46 us

profile of v4, /device:TPU:0, one launch (start us, length us, event | category | flops | bytes accessed | tf_op | source)
XLA Modules:
  0.0 48.1 jit_solution(8507211052883634414)
XLA Ops:
  1.3 46.0 %sampled_and_bases.1 = f32[2,256,256]{2,1,0:T(8,128)S(1)} custom-call(s32[2]{0:T(128)} %tile_hbm.1, s32[2]{0:T(128)} %bitcast.7, s32[2,16]{1,0:T(2,128)} %column_hbm.1, s32[1]{0:T(128)} %bitcast.4.rank_ref, bf16[512,4096]{1,0:T(8,128)(2,1)} %bitcast.5, bf16[8,128,256]{2,1,0:T(8,128)(2,1)} %bitcast.6, bf16[2,128,2048]{2,1,0:T(8,128)(2,1)} %child_ref.1), custom_call_target="tpu_custom_call" | custom-call | tf_op jit(solution)/shard_map/sampled_and_bases/pallas_call | solution.py:598
  47.3 0.8 %fusion = (f32[1,256,256]{2,1,0:T(8,128)}, f32[1,256,256]{2,1,0:T(8,128)}) fusion(f32[2,256,256]{2,1,0:T(8,128)S(1)} %sampled_and_bases.1), kind=kLoop, calls=%fused_computation | loop fusion | bytes 1048576 | tf_op jit(solution)/shard_map/unstack | solution.py:688

commit v5 on v4

--- a/solution.py
+++ b/solution.py
@@ -265,48 +265,45 @@
         arrived(h, omega[h].at[pl.ds(0, amount * piece)], n)
 
     def pair_up(h, row, col, i, n=1):
-        send(h, place(h, row, col, i, n), 12, to_p)
+        send(h, place(h, row, col, i, n), 8, to_p)
 
     def gather_own(h):
         own_loads[h].wait()
         for i in range(8 - via_z[h]):
-            send(h, place(h, r, c, i), i if i < 4 else 8, to_x)
-            send(h, place(h, r, c, 7 - i), 4 + i if i < 4 else 8, to_y)
+            send(h, place(h, r, c, i), min(i, 4), to_x)
+            send(h, place(h, r, c, 7 - i), min(i, 4), to_y)
         pair_up(h, r, c, 0, 8)
 
     def gather_near(h, i):
-        ref = place(h, r_x, c, i)
-        arrived(h, ref, i)
+        all_arrived(h, 2, i)
+        from_x, from_y = place(h, r_x, c, i), place(h, r, 1 - c, 7 - i)
         if i < via_z[h]:
-            send(h, ref, 9, to_z)
-        send(h, ref, 10 + i // 2, to_y)
+            send(h, from_x, 5, to_z)
+            send(h, from_y, 5, to_z)
+        send(h, from_x, 6 + i // 2, to_y)
+        send(h, from_y, 6 + i // 2, to_x)
         pair_up(h, r_x, c, i)
-        ref = place(h, r, 1 - c, 7 - i)
-        arrived(h, ref, 4 + i)
-        if i < via_z[h]:
-            send(h, ref, 9, to_z)
-        send(h, ref, 10 + i // 2, to_x)
         pair_up(h, r, 1 - c, 7 - i)
 
     def gather_rest(h):
         n = 4 - via_z[h]
-        all_arrived(h, 2 * n, 8)
+        all_arrived(h, 2 * n, 4)
         pair_up(h, r_x, c, 4, n)
         pair_up(h, r, 1 - c, 4 - n, n)
 
     def gather_z(h):
         n = via_z[h]
-        all_arrived(h, 2 * n, 9)
+        all_arrived(h, 2 * n, 5)
         pair_up(h, r_x, c, 8 - n, n)
         pair_up(h, r, 1 - c, 0, n)
 
     def gather_far(h, g):
-        all_arrived(h, 4, 10 + g)
+        all_arrived(h, 4, 6 + g)
         pair_up(h, r_x, 1 - c, 2 * g, 2)
         pair_up(h, r_x, 1 - c, 6 - 2 * g, 2)
 
     def gather_pair(h):
-        all_arrived(h, 32, 12)
+        all_arrived(h, 32, 8)
 
     def gather_sent():
         for h in range(2):
@@ -484,7 +481,7 @@
             last = jnp.where(label == wanted, n, last)
         return last
 
-    spots = [(r_x, 1 - c), (r_x, c), (r, 1 - c), (r, c)]
+    spots = [(r_x, 1 - c), (r, 1 - c), (r_x, c), (r, c)]
     lasts = [[last_of(row, col, j) for j in range(pieces)] for row, col in spots]
 
     gather_rest(1)
@@ -504,13 +501,13 @@
     def block(h, n, j):
         row, col = spots[n]
         total = sums[lasts[n][j]]
-        if n >= 2:
+        if n in (1, 3):
             at = pl.multiple_of(col * own_rows + j * 128, 128)
             total = total + part[h, pl.ds(at, 128), :]
         return total
 
     def hop(h, n):
-        target = (to_d, to_x, to_y)[n]
+        target = (to_d, to_y, to_x)[n]
         return rcopy(blocks.at[h, n], got.at[h, n], es.at[0], er.at[h], target)
 
     def spread(h):
@@ -619,7 +616,7 @@
             pltpu.VMEM((3, half, half), F32),
             dma(10),
             dma(2),
-            dma(2, 13),
+            dma(2, 9),
             dma(2),
             dma(3, 4),
             dma(2),

time: 48.3 us -> 48.3 us (level)
  no operation moved by 1% of the time
where the time goes in v5:
time: 48.3 us; the launch traced here: 48.1 us
  Pallas kernels  46 us (95%)
  between operations  1.29 us (3%)
  local copies, waits for them, and re-layouts  0.82 us (2%)
    pallas_call x1, Pallas kernels, sampled_and_bases(): pl.pallas_call(sample_kernel, out_shape=jax.ShapeDtypeStruct((2, rows, wi...  46 us

profile of v5, /device:TPU:0, one launch (start us, length us, event | category | flops | bytes accessed | tf_op | source)
XLA Modules:
  0.0 48.1 jit_solution(3316695791643662632)
XLA Ops:
  1.3 46.0 %sampled_and_bases.1 = f32[2,256,256]{2,1,0:T(8,128)S(1)} custom-call(s32[2]{0:T(128)} %tile_hbm.1, s32[2]{0:T(128)} %bitcast.7, s32[2,16]{1,0:T(2,128)} %column_hbm.1, s32[1]{0:T(128)} %bitcast.4.rank_ref, bf16[512,4096]{1,0:T(8,128)(2,1)} %bitcast.5, bf16[8,128,256]{2,1,0:T(8,128)(2,1)} %bitcast.6, bf16[2,128,2048]{2,1,0:T(8,128)(2,1)} %child_ref.1), custom_call_target="tpu_custom_call" | custom-call | tf_op jit(solution)/shard_map/sampled_and_bases/pallas_call | solution.py:595
  47.3 0.8 %fusion = (f32[1,256,256]{2,1,0:T(8,128)}, f32[1,256,256]{2,1,0:T(8,128)}) fusion(f32[2,256,256]{2,1,0:T(8,128)S(1)} %sampled_and_bases.1), kind=kLoop, calls=%fused_computation | loop fusion | bytes 1048576 | tf_op jit(solution)/shard_map/unstack | solution.py:685
